TPU v7x, 128 devices: a whole 4x4x4 slice. The times are simulated.
128 devices in a mesh: row: 8 (over z, core), col: 16 (over y, x).
Axes of the slice: x: 4, y: 4, z: 4, core: 2. Of those that a mesh axis runs over, the one named last changes fastest.
Arguments:
- inputs: bfloat16 [512, 8192], P('row', 'col'), may hold values from -6 to 6
- grad_out: bfloat16 [512, 8192], P('row', 'col'), may hold values from -0.1796875 to 0.1796875
- gate_pre: bfloat16 [512, 28672], P('col', 'row'), may hold values from -6 to 6
- up_pre: bfloat16 [512, 28672], P('col', 'row'), may hold values from -6 to 6
- w_gate: bfloat16 [8192, 28672], P('col', 'row'), may hold values from -0.25 to 0.25
- w_up: bfloat16 [8192, 28672], P('col', 'row'), may hold values from -0.25 to 0.25
- w_down: bfloat16 [28672, 8192], P('row', 'col'), may hold values from -0.03125 to 0.03125
Outputs:
- grad_inputs: bfloat16 [512, 8192], P('row', 'col')
- grad_gate: bfloat16 [8192, 28672], P('col', 'row')
- grad_up: bfloat16 [8192, 28672], P('col', 'row')
- grad_down: bfloat16 [28672, 8192], P('row', 'col')
All inputs are finite; a program needn't handle non-finite values.
Results may differ from a plain program's by a relative error of at most 0.005.
Values may be sent and summed in bfloat16 or wider, within the bound.
A program may use at most 128 MiB of HBM per device.

v0:
```python
import jax
import jax.numpy as jnp
from jax import lax
from jax.sharding import PartitionSpec as P


def swiglu_back(gate_pre, up_pre, hidden_grad):
    gate_wide = gate_pre.astype(jnp.float32)
    up_wide = up_pre.astype(jnp.float32)
    logistic = jax.nn.sigmoid(gate_wide)
    swished = gate_wide * logistic
    hidden = (swished * up_wide).astype(jnp.bfloat16)
    up_grad = (hidden_grad * swished).astype(jnp.bfloat16)
    gate_grad = (hidden_grad * up_wide * logistic * (1.0 + gate_wide * (1.0 - logistic))).astype(
        jnp.bfloat16
    )
    return (hidden, gate_grad, up_grad)


def on_device(inputs, grad_out, gate_pre, up_pre, w_gate, w_up, w_down):
    last_last = (((1,), (1,)), ((), ()))
    first_first = (((0,), (0,)), ((), ()))
    inputs_all, grad_out_all = (
        lax.all_gather(inputs, "row", axis=0, tiled=True),
        lax.all_gather(grad_out, "row", axis=0, tiled=True),
    )
    hidden_grad = lax.psum_scatter(
        lax.dot_general(grad_out_all, w_down, last_last, preferred_element_type=jnp.float32),
        "col",
        scatter_dimension=0,
        tiled=True,
    )
    hidden, gate_grad, up_grad = swiglu_back(gate_pre, up_pre, hidden_grad)
    hidden_all, gate_grad_all, up_grad_all = (
        lax.all_gather(hidden, "col", axis=0, tiled=True),
        lax.all_gather(gate_grad, "col", axis=0, tiled=True),
        lax.all_gather(up_grad, "col", axis=0, tiled=True),
    )
    grad_down = lax.dot_general(
        hidden_all, grad_out_all, first_first, preferred_element_type=jnp.float32
    ).astype(jnp.bfloat16)
    grad_gate = lax.dot_general(
        inputs_all, gate_grad_all, first_first, preferred_element_type=jnp.float32
    ).astype(jnp.bfloat16)
    grad_up = lax.dot_general(
        inputs_all, up_grad_all, first_first, preferred_element_type=jnp.float32
    ).astype(jnp.bfloat16)
    summed = lax.dot_general(gate_grad_all, w_gate, last_last, preferred_element_type=jnp.float32)
    grad_inputs = lax.psum_scatter(
        summed + lax.dot_general(up_grad_all, w_up, last_last, preferred_element_type=jnp.float32),
        "row",
        scatter_dimension=0,
        tiled=True,
    ).astype(jnp.bfloat16)
    return (grad_inputs, grad_gate, grad_up, grad_down)


def solution(mesh):
    placed = (
        P("row", "col"),
        P("row", "col"),
        P("col", "row"),
        P("col", "row"),
        P("col", "row"),
        P("col", "row"),
        P("row", "col"),
    )
    return jax.shard_map(
        on_device,
        mesh=mesh,
        in_specs=placed,
        out_specs=(P("row", "col"), P("col", "row"), P("col", "row"), P("row", "col")),
        check_vma=False,
    )
```

profile of v0, /device:TPU:1, one launch (start us, length us, event | category | flops | bytes accessed | tf_op | source)
XLA Modules:
  0.0 307.0 jit_solution(8646618759056539256)
XLA Ops:
  7.2 0.0 reduce-scatter.3.cloned.1.call-start
  7.2 15.9 %all_gather.15 = bf16[512,512]{1,0:T(8,128)(2,1)S(1)} all-gather(bf16[64,512]{1,0:T(8,128)(2,1)} %param.8), channel_id=1, replica_groups=mesh['row'=8,'col'=16] {'row'}, dimensions={0}, use_global_device_ids=true | all-gather | bytes 589824 | tf_op jit(solution)/shard_map/all_gather | solution.py:25
  23.1 7.1 %fusion.10 = f32[512,3584]{1,0:T(8,128)} fusion(bf16[512,512]{1,0:T(8,128)(2,1)S(1)} %all_gather.15, bf16[3584,512]{1,0:T(8,128)(2,1)} %param.13), kind=kOutput, calls=%fused_computation.20 | convolution fusion | flops 1879048192 | bytes 11534336 | tf_op jit(solution)/shard_map/dot_general | solution.py:28
  30.2 0.0 copy-start
  30.2 0.0 copy-start.1
  30.2 0.0 reduce-scatter.3.cloned.1.call-update
  30.2 0.0 all-gather.4.cloned.1.call-start
  30.2 82.3 %reduce-scatter.3.cloned.1.call-done = f32[32,3584]{1,0:T(8,128)} async-done(((f32[512,3584]{1,0:T(8,128)}), f32[32,3584]{1,0:T(8,128)}) %reduce-scatter.3.cloned.1.call-update) | async-done | bytes 458768 | tf_op jit(solution)/shard_map/reduce_scatter | solution.py:27
  112.6 0.0 copy-done
  112.6 0.0 copy-done.1
  112.6 2.1 multiply_convert_fusion
  114.6 0.0 all-gather.4.cloned.1.call-update
  114.7 0.0 all-gather.6.cloned.1.call-start
  114.7 0.7 all-gather.6.cloned.1.call-update
  115.4 0.0 all-gather.8.cloned.1.call-start
  115.4 0.5 all-gather.8.cloned.1.call-update
  116.0 0.0 reduce-scatter.5.cloned.1.call-start
  116.0 49.2 %all-gather.4.cloned.1.call-done = bf16[512,3584]{1,0:T(8,128)(2,1)} async-done(((bf16[32,3584]{1,0:T(8,128)(2,1)}), bf16[512,3584]{1,0:T(8,128)(2,1)}) %all-gather.4.cloned.1.call-update) | async-done | bytes 3670032 | tf_op jit(solution)/shard_map/all_gather | solution.py:36
  165.2 5.2 %fusion.11 = f32[512,512]{1,0:T(8,128)S(1)} fusion(bf16[512,3584]{1,0:T(8,128)(2,1)} %all-gather.4.cloned.1.call-done, bf16[512,3584]{1,0:T(8,128)(2,1)} %param.11), kind=kOutput, calls=%fused_computation.21 | convolution fusion | flops 1879048192 | bytes 8388608 | tf_op jit(solution)/shard_map/dot_general | solution.py:48
  170.4 0.0 copy-start.2
  170.5 46.5 %all-gather.6.cloned.1.call-done = bf16[512,3584]{1,0:T(8,128)(2,1)} async-done(((bf16[32,3584]{1,0:T(8,128)(2,1)}), bf16[512,3584]{1,0:T(8,128)(2,1)}) %all-gather.6.cloned.1.call-update) | async-done | bytes 3670032 | tf_op jit(solution)/shard_map/all_gather | solution.py:37
  216.9 6.2 %convolution_add_fusion = f32[512,512]{1,0:T(8,128)} fusion(f32[512,512]{1,0:T(8,128)S(1)} %fusion.11, bf16[512,3584]{1,0:T(8,128)(2,1)} %all-gather.6.cloned.1.call-done, bf16[512,3584]{1,0:T(8,128)(2,1)} %param.12), kind=kOutput, calls=%fused_computation.5 | convolution fusion | flops 1879310336 | bytes 9437184 | tf_op jit(solution)/shard_map/dot_general | solution.py:50
  223.2 0.0 reduce-scatter.5.cloned.1.call-update
  223.2 0.0 copy-done.2
  223.2 14.7 %all_gather.18 = bf16[512,512]{1,0:T(8,128)(2,1)S(1)} all-gather(bf16[64,512]{1,0:T(8,128)(2,1)S(1)} %copy-done.2), channel_id=1, replica_groups=mesh['row'=8,'col'=16] {'row'}, dimensions={0}, use_global_device_ids=true | all-gather | bytes 589824 | tf_op jit(solution)/shard_map/all_gather | solution.py:24
  237.9 6.0 %fusion = bf16[512,3584]{0,1:T(8,128)(2,1)} fusion(bf16[512,3584]{1,0:T(8,128)(2,1)} %all-gather.4.cloned.1.call-done, bf16[512,512]{1,0:T(8,128)(2,1)S(1)} %all_gather.18), kind=kOutput, calls=%fused_computation.3 | convolution fusion | flops 1880883200 | bytes 7864320 | tf_op jit(solution)/shard_map/dot_general | solution.py:42
  243.9 5.9 %copy.11 = bf16[512,3584]{1,0:T(8,128)(2,1)} copy(bf16[512,3584]{0,1:T(8,128)(2,1)} %fusion) | data formatting | bytes 7340032
  249.8 6.0 %fusion.1 = bf16[512,3584]{0,1:T(8,128)(2,1)} fusion(bf16[512,3584]{1,0:T(8,128)(2,1)} %all-gather.6.cloned.1.call-done, bf16[512,512]{1,0:T(8,128)(2,1)S(1)} %all_gather.18), kind=kOutput, calls=%fused_computation.4 | convolution fusion | flops 1880883200 | bytes 7864320 | tf_op jit(solution)/shard_map/dot_general | solution.py:45
  255.8 6.0 %copy.12 = bf16[512,3584]{1,0:T(8,128)(2,1)} copy(bf16[512,3584]{0,1:T(8,128)(2,1)} %fusion.1) | data formatting | bytes 7340032
  261.8 6.2 %all-gather.8.cloned.1.call-done = bf16[512,3584]{1,0:T(8,128)(2,1)} async-done(((bf16[32,3584]{1,0:T(8,128)(2,1)}), bf16[512,3584]{1,0:T(8,128)(2,1)}) %all-gather.8.cloned.1.call-update) | async-done | bytes 3670032 | tf_op jit(solution)/shard_map/all_gather | solution.py:35
  268.0 6.0 %convolution_convert_fusion = bf16[3584,512]{1,0:T(8,128)(2,1)} fusion(bf16[512,3584]{1,0:T(8,128)(2,1)} %all-gather.8.cloned.1.call-done, bf16[512,512]{1,0:T(8,128)(2,1)S(1)} %all_gather.15), kind=kOutput, calls=%fused_computation | convolution fusion | flops 1880883200 | bytes 7864320 | tf_op jit(solution)/shard_map/dot_general | solution.py:39
  273.9 25.0 %reduce-scatter.5.cloned.1.call-done = f32[64,512]{1,0:T(8,128)} async-done(((f32[512,512]{1,0:T(8,128)}), f32[64,512]{1,0:T(8,128)}) %reduce-scatter.5.cloned.1.call-update) | async-done | bytes 131088 | tf_op jit(solution)/shard_map/reduce_scatter | solution.py:49
  299.0 1.5 convert_element_type.37
Async XLA Ops:
  7.2 105.4 %reduce-scatter.3.cloned.1.call-start = ((), (), s32[]{:S(2)}) async-start(), calls=%async_computation.2 | async-start | bytes 7798784 | tf_op jit(solution)/shard_map/reduce_scatter | solution.py:27
  30.2 82.4 %copy-start = (bf16[32,3584]{1,0:T(8,128)(2,1)S(1)}, bf16[32,3584]{1,0:T(8,128)(2,1)}, u32[]{:S(2)}) copy-start(bf16[32,3584]{1,0:T(8,128)(2,1)} %param.9) | copy-start | bytes 688132
  30.2 82.4 %copy-start.1 = (bf16[32,3584]{1,0:T(8,128)(2,1)S(1)}, bf16[32,3584]{1,0:T(8,128)(2,1)}, u32[]{:S(2)}) copy-start(bf16[32,3584]{1,0:T(8,128)(2,1)} %param.10) | copy-start | bytes 688132
  30.2 135.0 %all-gather.4.cloned.1.call-start = ((), (), s32[]{:S(2)}) async-start(), calls=%async_computation.3 | async-start | bytes 3899392 | tf_op jit(solution)/shard_map/all_gather | solution.py:36
  114.7 102.3 %all-gather.6.cloned.1.call-start = ((), (), s32[]{:S(2)}) async-start(), calls=%async_computation.4 | async-start | bytes 3899392 | tf_op jit(solution)/shard_map/all_gather | solution.py:37
  115.4 152.6 %all-gather.8.cloned.1.call-start = ((), (), s32[]{:S(2)}) async-start(), calls=%async_computation.6 | async-start | bytes 3899392 | tf_op jit(solution)/shard_map/all_gather | solution.py:35
  116.0 183.0 %reduce-scatter.5.cloned.1.call-start = ((), (), s32[]{:S(2)}) async-start(), calls=%async_computation.5 | async-start | bytes 1179648 | tf_op jit(solution)/shard_map/reduce_scatter | solution.py:49
  170.4 52.7 %copy-start.2 = (bf16[64,512]{1,0:T(8,128)(2,1)S(1)}, bf16[64,512]{1,0:T(8,128)(2,1)}, u32[]{:S(2)}) copy-start(bf16[64,512]{1,0:T(8,128)(2,1)} %param.7) | copy-start | bytes 196612
Sparse Core Ops, SparseCore 0:
  30.3 82.2 reduce-scatter.2
  115.5 49.6 all-gather.3
  168.1 48.7 all-gather.5
  219.2 48.7 all-gather.7
  270.3 28.6 reduce-scatter.4
where the time goes:
time: 310 us; the launch traced here: 307 us
  waiting for transfers between devices  210 us (68%)
  matrix products  36.5 us (12%)
  blocking collectives  30.5 us (10%)
  between operations  13.8 us (4%)
  local copies, waits for them, and re-layouts  11.9 us (4%)
  other arithmetic  3.61 us (1%)
    reduce_scatter x1, waiting for transfers between devices, on_device(): lax.psum_scatter(lax.dot_general(grad_out_all, w_down, last_last, preferr...  82.3 us
    all_gather x1, waiting for transfers between devices, on_device(): lax.all_gather(gate_grad, 'col', axis=0, tiled=True)  49.2 us
    all_gather x1, waiting for transfers between devices, on_device(): lax.all_gather(up_grad, 'col', axis=0, tiled=True)  46.5 us
    reduce_scatter x1, waiting for transfers between devices, on_device(): lax.psum_scatter(summed + lax.dot_general(up_grad_all, w_up, last_last, p...  25 us
    all_gather x1, blocking collectives, on_device(): lax.all_gather(grad_out, 'row', axis=0, tiled=True)  15.9 us
    all_gather x1, blocking collectives, on_device(): lax.all_gather(inputs, 'row', axis=0, tiled=True)  14.7 us
    unnamed x8, local copies, waits for them, and re-layouts  11.9 us
    dot_general x1, matrix products, on_device(): lax.dot_general(grad_out_all, w_down, last_last, preferred_element_type=j...  7.08 us
  transfers between devices with their start and end apart: 5, of which 5 were waited for; matrix products, arithmetic and copies ran while one was open for 13% of the time, Pallas kernels for 0%

commit v1 on v0

v1 whole, which is shorter than its diff:
```python
import jax
import jax.numpy as jnp
from jax import lax
from jax.experimental import pallas as pl
from jax.experimental.pallas import tpu as pltpu
from jax.sharding import PartitionSpec as P

MESH = pl.DeviceIdType.MESH
F32, BF16 = jnp.float32, jnp.bfloat16
NT = (((1,), (1,)), ((), ()))
TN = (((0,), (0,)), ((), ()))
R = 4
TB = 32
FFS = 3584
HALF = FFS // 2
QUART = FFS // 4
DS = 512
RB = 64
T2 = F32


def cols(h, q):
    return pl.ds(h * HALF + q * QUART, QUART)


def comm_kernel(
    inp_ref, go_ref, gp_ref, up_ref, wg_ref, wu_ref, wd_ref,
    hid_out, gg_out, ug_out, inp_out, go_out, gi_out,
    g_all, inp_all, go_all, gp, up, wg, wu, wd,
    p32, p16, r1, s1, m32, r2, s2, acc, sib, tot, zin, gi,
    loc, ss, rs,
):
    col, row = lax.axis_index("col"), lax.axis_index("row")
    y, x = col // R, lax.rem(col, R)
    z, core = row // 2, lax.rem(row, 2)

    def add(p, k):
        return lax.rem(p + k, R)

    def at(axis, k):
        return {"col": y * R + add(x, k)} if axis == "x" else {"col": add(y, k) * R + x}

    zdev = [{"row": add(z, k) * 2 + core} for k in (1, 2, 3)]
    other = {"row": z * 2 + 1 - core}

    def rc(k, src, dst, dev):
        return pltpu.make_async_remote_copy(
            src_ref=src, dst_ref=dst, send_sem=ss.at[k], recv_sem=rs.at[k], device_id=dev, device_id_type=MESH
        )

    def got(k, ref):
        rc(k, ref, ref, other).wait_recv()

    def sent(k, ref):
        rc(k, ref, ref, other).wait_send()

    def lc(k, src, dst):
        return pltpu.make_async_copy(src, dst, loc.at[k])

    loads = [
        lc(0, go_ref, go_all.at[row]), lc(1, gp_ref, gp), lc(2, up_ref, up), lc(3, wd_ref, wd),
        lc(4, inp_ref, inp_all.at[row]), lc(5, wg_ref, wg), lc(6, wu_ref, wu),
    ]
    for c in loads:
        c.start()

    barrier = pltpu.get_barrier_semaphore()
    peers = [at("x", 1), at("x", 3), at("y", 1), at("y", 3), other] + zdev
    for d in peers:
        pl.semaphore_signal(barrier, inc=1, device_id=d, device_id_type=MESH)
    pl.semaphore_wait(barrier, len(peers))

    class RowGather:
        def __init__(self, base, ref):
            self.b, self.ref = base, ref

        def start(self):
            for i in range(3):
                rc(self.b + i, self.ref.at[row], self.ref.at[row], zdev[i]).start()
            rc(self.b + 3, self.ref.at[row], self.ref.at[row], other).start()

        def src(self, i):
            return self.ref.at[add(z, 3 - i) * 2 + core]

        def forward(self):
            for i in range(3):
                got(self.b + i, self.src(i))
                rc(self.b + 4 + i, self.src(i), self.src(i), other).start()

        def finish(self):
            for i in range(3, 7):
                got(self.b + i, self.ref.at[row])
            for i in range(7):
                sent(self.b + i, self.ref.at[row])

    class Gather:
        def __init__(self, base, axis, view):
            self.b, self.axis, self.view = base, axis, view
            self.me = x if axis == "x" else y

        def start(self):
            b, v, me = self.b, self.view, self.me
            for k, q, step in ((0, 0, 1), (1, 1, 3), (2, 1, 1), (3, 0, 3)):
                rc(b + k, v(me, q), v(me, q), at(self.axis, step)).start()

        def forward(self):
            b, v, me = self.b, self.view, self.me
            got(b, v(add(me, 3), 0))
            rc(b + 4, v(add(me, 3), 0), v(add(me, 3), 0), at(self.axis, 1)).start()
            got(b + 1, v(add(me, 1), 1))
            rc(b + 5, v(add(me, 1), 1), v(add(me, 1), 1), at(self.axis, 3)).start()

        def near(self):
            got(self.b + 2, self.view(add(self.me, 3), 1))
            got(self.b + 3, self.view(add(self.me, 1), 0))

        def far(self):
            got(self.b + 4, self.view(add(self.me, 2), 0))
            got(self.b + 5, self.view(add(self.me, 2), 1))

        def drain(self):
            for k in range(6):
                sent(self.b + k, self.view(self.me, 0))

    def gathers(base, a, h):
        g = g_all.at[a]
        if h == 0:
            first = Gather(base, "x", lambda p, q: g.at[y, p, :, cols(h, q)])
            second = Gather(base + 6, "y", lambda p, q: g.at[p, :, :, cols(h, q)])
        else:
            first = Gather(base, "y", lambda p, q: g.at[p, x, :, cols(h, q)])
            second = Gather(base + 6, "x", lambda p, q: g.at[:, p, :, cols(h, q)])
        return first, second

    class Scatter:
        def __init__(self, base, axis, wide, narrow, recv, send):
            self.b, self.axis, self.wide, self.narrow, self.recv, self.send = base, axis, wide, narrow, recv, send
            self.me = x if axis == "x" else y

        def start(self):
            me = self.me
            for k, d, q, step in ((0, 2, 0, 1), (1, 2, 1, 3), (2, 1, 1, 1), (3, 3, 0, 3)):
                rc(self.b + k, self.narrow(add(me, d), q), self.recv.at[k], at(self.axis, step)).start()

        def forward(self):
            me = self.me
            for k, d, q, step in ((0, 1, 0, 1), (1, 3, 1, 3)):
                got(self.b + k, self.recv.at[k])
                part = self.wide(add(me, d), q)[...] + self.recv[k].astype(F32)
                self.send[k] = part.astype(self.send.dtype)
                rc(self.b + 4 + k, self.send.at[k], self.recv.at[4 + k], at(self.axis, step)).start()

        def result(self, q):
            k = (3, 4) if q == 0 else (2, 5)
            got(self.b + k[0], self.recv.at[k[0]])
            got(self.b + k[1], self.recv.at[k[1]])
            return self.wide(self.me, q)[...] + self.recv[k[0]].astype(F32) + self.recv[k[1]].astype(F32)

        def drain(self):
            for k in range(6):
                sent(self.b + k, self.recv.at[0])

    go_gather, inp_gather = RowGather(0, go_all), RowGather(7, inp_all)
    hid = [gathers(14 + 12 * h, 0, h) for h in range(2)]
    ggs = [gathers(38 + 12 * h, 1, h) for h in range(2)]
    ugs = [gathers(62 + 12 * h, 2, h) for h in range(2)]
    red1 = [
        Scatter(86, "y", lambda d, q: p32.at[d, :, :, cols(0, q)], lambda d, q: p16.at[d, :, :, cols(0, q)], r1.at[0], s1.at[0]),
        Scatter(92, "x", lambda d, q: p32.at[:, d, :, cols(1, q)], lambda d, q: p16.at[:, d, :, cols(1, q)], r1.at[1], s1.at[1]),
    ]
    red2 = [
        Scatter(98 + 6 * h, "xy"[h], lambda d, q, h=h: m32.at[h, q, d], lambda d, q, h=h: m32.at[h, q, d], r2.at[h], s2.at[h])
        for h in range(2)
    ]
    ROWSUM = 110

    loads[0].wait()
    go_gather.start()
    loads[4].wait()
    inp_gather.start()

    loads[1].wait()
    loads[2].wait()
    gw, uw = gp[...].astype(F32), up[...].astype(F32)
    g_all[0, y, x] = (gw * jax.nn.sigmoid(gw) * uw).astype(BF16)
    for f, s in hid:
        f.start()

    go_gather.forward()
    for f, s in hid:
        f.forward()
    go_gather.finish()
    loads[3].wait()

    def product(i, c):
        at_ = pl.ds(pl.multiple_of(i * 256, 256), 256)
        t = lax.dot_general(go_all[...].reshape(512, DS), wd[at_, :], NT, preferred_element_type=F32).reshape(R, R, TB, 256)
        p32[:, :, :, at_] = t
        p16[:, :, :, at_] = t.astype(BF16)
        return c

    lax.fori_loop(0, FFS // 256, product, 0)
    for r in red1:
        r.start()
    for f, s in hid:
        f.near()
        f.far()
    for r in red1:
        r.forward()
    for f, s in hid:
        s.start()
    inp_gather.forward()
    for h in range(2):
        for q in range(2):
            m32[h, q] = red1[h].result(q)
        red2[h].start()
    for h in range(2):
        red2[h].forward()
    for f, s in hid:
        s.forward()
    for h in range(2):
        for q in range(2):
            c = cols(h, q)
            hg = red2[h].result(q)
            gw, uw = gp[:, c].astype(F32), up[:, c].astype(F32)
            sg = jax.nn.sigmoid(gw)
            g_all[1, y, x, :, c] = (hg * uw * sg * (1.0 + gw * (1.0 - sg))).astype(BF16)
            g_all[2, y, x, :, c] = (hg * (gw * sg)).astype(BF16)
        ggs[h][0].start()
        ugs[h][0].start()
    for f, s in hid:
        s.near()
        s.far()
    save_h = lc(7, g_all.at[0], hid_out)
    save_h.start()
    for h in range(2):
        ggs[h][0].forward()
        ugs[h][0].forward()
    inp_gather.finish()
    save_i = lc(8, inp_all, inp_out)
    save_i.start()
    save_g = lc(9, go_all, go_out)
    save_g.start()
    for group in (ggs, ugs):
        for h in range(2):
            group[h][0].near()
            group[h][0].far()
            group[h][1].start()
    loads[5].wait()
    loads[6].wait()
    for group in (ggs, ugs):
        for h in range(2):
            group[h][1].forward()
    acc[...] = jnp.zeros_like(acc)

    def bundle(h, p):
        def piece(a, w):
            def body(i, t):
                c = pl.ds(pl.multiple_of(h * HALF + i * 256, 256), 256)
                lhs = g_all[a, p, :, :, c] if h == 0 else g_all[a, :, p, :, c]
                return t + lax.dot_general(lhs.reshape(R * TB, 256), w[:, c], NT, preferred_element_type=F32)

            return body

        t = jnp.zeros((R * TB, DS), F32)
        t = lax.fori_loop(0, HALF // 256, piece(1, wg), t)
        t = lax.fori_loop(0, HALF // 256, piece(2, wu), t).reshape(R, TB, DS)
        if h == 0:
            acc[p] += t
        else:
            acc[:, p] += t

    for h in range(2):
        bundle(h, (y, x)[h])
    for group in (ggs, ugs):
        for h in range(2):
            group[h][1].near()
    for h in range(2):
        for k in (1, 3):
            bundle(h, add((y, x)[h], k))
    for group in (ggs, ugs):
        for h in range(2):
            group[h][1].far()
    save_gg = lc(10, g_all.at[1], gg_out)
    save_gg.start()
    save_ug = lc(11, g_all.at[2], ug_out)
    save_ug.start()
    for h in range(2):
        bundle(h, add((y, x)[h], 2))

    rc(ROWSUM, acc.at[:, pl.ds(2 * (1 - core), 2)], sib, other).start()
    got(ROWSUM, sib)
    tot[...] = acc[:, pl.ds(2 * core, 2)] + sib[...]
    for i in range(3):
        rc(ROWSUM + 1 + i, tot.at[add(z, 1 + i)], zin.at[i], zdev[i]).start()
    total = tot[z]
    for i in range(3):
        got(ROWSUM + 1 + i, zin.at[i])
        total = total + zin[i]
    gi[...] = total.reshape(RB, DS).astype(BF16)
    save = lc(12, gi, gi_out)
    save.start()

    for group in (hid, ggs, ugs):
        for f, s in group:
            f.drain()
            s.drain()
    for r in red1 + red2:
        r.drain()
    sent(ROWSUM, sib)
    for i in range(3):
        sent(ROWSUM + 1 + i, zin.at[i])
    for c in (save_h, save_i, save_g, save_gg, save_ug, save):
        c.wait()


def weights_kernel(inp_ref, go_ref, hid_ref, gg_ref, ug_ref, dg_ref, du_ref, dd_ref):
    def rows(ref):
        return ref[...].reshape(512, ref.shape[-1])

    inp, go = rows(inp_ref), rows(go_ref)
    dg_ref[...] = lax.dot_general(inp, rows(gg_ref), TN, preferred_element_type=F32).astype(BF16)
    du_ref[...] = lax.dot_general(inp, rows(ug_ref), TN, preferred_element_type=F32).astype(BF16)
    dd_ref[...] = lax.dot_general(rows(hid_ref), go, TN, preferred_element_type=F32).astype(BF16)


def on_device(inputs, grad_out, gate_pre, up_pre, w_gate, w_up, w_down):
    anywhere = pl.BlockSpec(memory_space=pl.ANY)
    block = jax.ShapeDtypeStruct((R, R, TB, FFS), BF16)
    tokens = jax.ShapeDtypeStruct((2 * R, RB, DS), BF16)
    hidden, gate_grad, up_grad, inp_all, go_all, grad_inputs = pl.pallas_call(
        comm_kernel,
        out_shape=(block, block, block, tokens, tokens, jax.ShapeDtypeStruct((RB, DS), BF16)),
        in_specs=[anywhere] * 7,
        out_specs=[anywhere] * 6,
        scratch_shapes=[
            pltpu.VMEM((3, R, R, TB, FFS), BF16),
            pltpu.VMEM((2 * R, RB, DS), BF16),
            pltpu.VMEM((2 * R, RB, DS), BF16),
            pltpu.VMEM((TB, FFS), BF16),
            pltpu.VMEM((TB, FFS), BF16),
            pltpu.VMEM((DS, FFS), BF16),
            pltpu.VMEM((DS, FFS), BF16),
            pltpu.VMEM((FFS, DS), BF16),
            pltpu.VMEM((R, R, TB, FFS), F32),
            pltpu.VMEM((R, R, TB, FFS), BF16),
            pltpu.VMEM((2, 6, R, TB, QUART), BF16),
            pltpu.VMEM((2, 2, R, TB, QUART), BF16),
            pltpu.VMEM((2, 2, R, TB, QUART), F32),
            pltpu.VMEM((2, 6, TB, QUART), T2),
            pltpu.VMEM((2, 2, TB, QUART), T2),
            pltpu.VMEM((R, R, TB, DS), F32),
            pltpu.VMEM((R, 2, TB, DS), F32),
            pltpu.VMEM((R, 2, TB, DS), F32),
            pltpu.VMEM((3, 2, TB, DS), F32),
            pltpu.VMEM((RB, DS), BF16),
            pltpu.SemaphoreType.DMA((13,)),
            pltpu.SemaphoreType.DMA((114,)),
            pltpu.SemaphoreType.DMA((114,)),
        ],
        compiler_params=pltpu.CompilerParams(
            collective_id=0, has_side_effects=True, vmem_limit_bytes=60 * 1024 * 1024
        ),
    )(inputs, grad_out, gate_pre, up_pre, w_gate, w_up, w_down)

    tile = 512
    wide = pl.BlockSpec((R, R, TB, tile), lambda i: (0, 0, 0, i))
    whole = pl.BlockSpec((2 * R, RB, DS), lambda i: (0, 0, 0))
    grad_gate, grad_up, grad_down = pl.pallas_call(
        weights_kernel,
        grid=(FFS // tile,),
        out_shape=(
            jax.ShapeDtypeStruct((DS, FFS), BF16),
            jax.ShapeDtypeStruct((DS, FFS), BF16),
            jax.ShapeDtypeStruct((FFS, DS), BF16),
        ),
        in_specs=[whole, whole, wide, wide, wide],
        out_specs=[
            pl.BlockSpec((DS, tile), lambda i: (0, i)),
            pl.BlockSpec((DS, tile), lambda i: (0, i)),
            pl.BlockSpec((tile, DS), lambda i: (i, 0)),
        ],
        compiler_params=pltpu.CompilerParams(vmem_limit_bytes=48 * 1024 * 1024),
    )(inp_all, go_all, hidden, gate_grad, up_grad)
    return (grad_inputs, grad_gate, grad_up, grad_down)


def solution(mesh):
    placed = (
        P("row", "col"),
        P("row", "col"),
        P("col", "row"),
        P("col", "row"),
        P("col", "row"),
        P("col", "row"),
        P("row", "col"),
    )
    return jax.shard_map(
        on_device,
        mesh=mesh,
        in_specs=placed,
        out_specs=(P("row", "col"), P("col", "row"), P("col", "row"), P("row", "col")),
        check_vma=False,
    )
```

time: 310 us -> 142 us (0.46)
  waiting for transfers between devices: 210 us -> 0 us
  Pallas kernels: 0 us -> 136 us
  matrix products: 36.5 us -> 0 us
  blocking collectives: 30.5 us -> 0 us
  between operations: 13.8 us -> 0.65 us
  local copies, waits for them, and re-layouts: 11.9 us -> 4.75 us
  other arithmetic: 3.61 us -> 0 us
    pallas_call x0 -> x2, Pallas kernels: none -> 136 us  [the longest x1 125 us: on_device(): pl.pallas_call(comm_kernel, out_shape=(block, block, block, tokens, token...]
    reduce_scatter x2 -> x0, waiting for transfers between devices: 107 us -> none  [the longest x1 82.3 us: on_device(): lax.psum_scatter(lax.dot_general(grad_out_all, w_down, last_last, preferr...]
    all_gather x3 -> x0, waiting for transfers between devices: 102 us -> none  [the longest x1 49.2 us: on_device(): lax.all_gather(gate_grad, 'col', axis=0, tiled=True)]
    dot_general x6 -> x0, matrix products: 36.5 us -> none  [the longest x1 7.08 us: on_device(): lax.dot_general(grad_out_all, w_down, last_last, preferred_element_type=j...]
    all_gather x2 -> x0, blocking collectives: 30.5 us -> none  [the longest x1 15.9 us: on_device(): lax.all_gather(grad_out, 'row', axis=0, tiled=True)]
    unnamed x8 -> x9, local copies, waits for them, and re-layouts: 11.9 us -> 4.75 us
    convert_element_type x2 -> x0, other arithmetic: 3.61 us -> none  [the longest x1 2.07 us: swiglu_back(): up_grad = (hidden_grad * swished).astype(jnp.bfloat16)]
  transfers between devices with their start and end apart: 5 -> 0, of which waited for: 5 -> 0; matrix products, arithmetic and copies ran while one was open for 13% -> 0% of each run, Pallas kernels for 0% -> 0%
where the time goes in v1:
time: 142 us; the launch traced here: 141 us
  Pallas kernels  136 us (96%)
  local copies, waits for them, and re-layouts  4.75 us (3%)
    pallas_call x1, Pallas kernels, on_device(): pl.pallas_call(comm_kernel, out_shape=(block, block, block, tokens, token...  125 us
    pallas_call x1, Pallas kernels, on_device(): pl.pallas_call(weights_kernel, grid=(FFS // tile,), out_shape=(jax.ShapeD...  10.7 us
    unnamed x9, local copies, waits for them, and re-layouts  4.75 us

profile of v1, /device:TPU:1, one launch (start us, length us, event | category | flops | bytes accessed | tf_op | source)
XLA Modules:
  0.0 141.2 jit_solution(4297246391094472513)
XLA Ops:
  0.6 125.1 %shard_map.102 = (bf16[4,4,32,3584]{3,2,1,0:T(8,128)(2,1)}, bf16[4,4,32,3584]{3,2,1,0:T(8,128)(2,1)}, bf16[4,4,32,3584]{3,2,1,0:T(8,128)(2,1)}, bf16[8,64,512]{2...) custom-call(bf16[64,512]{1,0:T(8,128)(2,1)} %inp_ref.1, bf16[64,512]{1,0:T(8,128)(2,1)} %go_ref.1, ...), custom_call_target="tpu_custom_call" | custom-call | tf_op jit(solution)/shard_map/pallas_call | solution.py:331
  125.7 0.0 copy-start
  125.8 2.0 %copy-done = bf16[4,4,32,3584]{3,2,1,0:T(8,128)(2,1)S(1)} copy-done((bf16[4,4,32,3584]{3,2,1,0:T(8,128)(2,1)S(1)}, bf16[4,4,32,3584]{3,2,1,0:T(8,128)(2,1)}, u32[]{:S(2)}) %copy-start) | copy-done | bytes 3670040
  127.8 0.0 copy-start.1
  127.8 1.0 copy-done.1
  128.8 0.0 copy-start.2
  128.8 1.0 copy-done.2
  129.9 0.0 copy-start.3
  129.9 10.7 %shard_map.103 = (bf16[512,3584]{1,0:T(8,128)(2,1)}, bf16[512,3584]{1,0:T(8,128)(2,1)}, bf16[3584,512]{1,0:T(8,128)(2,1)}) custom-call(bf16[8,64,512]{2,1,0:T(8,128)(2,1)S(1)} %copy-done.1, bf16[8,64,512]{2,1,0:T(8,128)(2,1)S(1)} %copy-done.2, bf16[4,4,32,3584]{3,2,1,0:T(8,128)(2,1)S(1)} %copy-done, bf16[4,4,32,3584]{3,2,1,0:T(8,128)(2,1)} %get-tuple-element.17.gg_ref, ...), custom_call_target="tpu_custom_call" | custom-call | tf_op jit(solution)/shard_map/pallas_call | solution.py:369
  140.6 0.0 copy-done.3
  140.6 0.6 copy.12
Async XLA Ops:
  125.7 2.0 %copy-start = (bf16[4,4,32,3584]{3,2,1,0:T(8,128)(2,1)S(1)}, bf16[4,4,32,3584]{3,2,1,0:T(8,128)(2,1)}, u32[]{:S(2)}) copy-start(bf16[4,4,32,3584]{3,2,1,0:T(8,128)(2,1)} %get-tuple-element.16.hid_ref) | copy-start | bytes 11010052
  127.8 1.0 copy-start.1
  128.8 1.0 copy-start.2
  129.9 10.7 %copy-start.3 = (bf16[64,512]{1,0:T(8,128)(2,1)S(1)}, bf16[64,512]{1,0:T(8,128)(2,1)}, u32[]{:S(2)}) copy-start(bf16[64,512]{1,0:T(8,128)(2,1)} %get-tuple-element.26) | copy-start | bytes 196612

commit v2 on v0

v2 whole, which is shorter than its diff:
```python
import jax
import jax.numpy as jnp
from jax import lax
from jax.experimental import pallas as pl
from jax.experimental.pallas import tpu as pltpu
from jax.sharding import PartitionSpec as P

MESH = pl.DeviceIdType.MESH
F32, BF16 = jnp.float32, jnp.bfloat16
NT = (((1,), (1,)), ((), ()))
TN = (((0,), (0,)), ((), ()))
R = 4
TB = 32
FFS = 3584
HALF = FFS // 2
QR = TB // 2
DS = 512
RB = 64
T2 = F32


CHUNKS = (4, 4, 3, 3)
LAG = 1
HIDDEN = (0, 1, 4, 7)


def comm_kernel(
    inp_ref, go_ref, gp_ref, up_ref, wg_ref, wu_ref, wd_ref,
    hid_all, g_all, inp_all, go_all, own, to1, to2, to3,
    gp, up, wg, wu, wd,
    p32, p16, r1, s1, m32, r2, s2, acc, sib,
    loc, ss, rs,
):
    col, row = lax.axis_index("col"), lax.axis_index("row")
    y, x = col // R, lax.rem(col, R)
    z, core = row // 2, lax.rem(row, 2)
    sems = [0]

    def take(n):
        sems[0] += n
        return sems[0] - n

    def add(p, k):
        return lax.rem(p + k, R)

    def at(axis, k):
        return {"col": y * R + add(x, k)} if axis == "x" else {"col": add(y, k) * R + x}

    zdev = [{"row": add(z, k) * 2 + core} for k in (1, 2, 3)]
    other = {"row": z * 2 + 1 - core}

    def rc(k, src, dst, dev):
        return pltpu.make_async_remote_copy(
            src_ref=src, dst_ref=dst, send_sem=ss.at[k], recv_sem=rs.at[k], device_id=dev, device_id_type=MESH
        )

    def got(k, ref):
        rc(k, ref, ref, other).wait_recv()

    def sent(k, ref):
        rc(k, ref, ref, other).wait_send()

    def lc(k, src, dst):
        return pltpu.make_async_copy(src, dst, loc.at[k])

    loads = [
        lc(0, go_ref, go_all.at[row]), lc(1, gp_ref, gp), lc(2, up_ref, up), lc(3, wd_ref, wd),
        lc(4, inp_ref, inp_all.at[row]), lc(5, wg_ref, wg), lc(6, wu_ref, wu),
    ]
    for c in loads:
        c.start()

    barrier = pltpu.get_barrier_semaphore()
    peers = [at("x", 1), at("x", 3), at("y", 1), at("y", 3), other] + zdev
    for d in peers:
        pl.semaphore_signal(barrier, inc=1, device_id=d, device_id_type=MESH)
    pl.semaphore_wait(barrier, len(peers))

    class RowGather:
        def __init__(self, ref):
            self.b, self.ref = take(7), ref

        def start(self):
            for i in range(3):
                rc(self.b + i, self.ref.at[row], self.ref.at[row], zdev[i]).start()
            rc(self.b + 3, self.ref.at[row], self.ref.at[row], other).start()

        def src(self, i):
            return self.ref.at[add(z, 3 - i) * 2 + core]

        def forward(self):
            for i in range(3):
                got(self.b + i, self.src(i))
                rc(self.b + 4 + i, self.src(i), self.src(i), other).start()

        def finish(self):
            for i in range(3, 7):
                got(self.b + i, self.ref.at[row])
            for i in range(7):
                sent(self.b + i, self.ref.at[row])

    class Gather:
        def __init__(self, axis, view):
            self.b, self.axis, self.view = take(6), axis, view
            self.me = x if axis == "x" else y

        def start(self):
            b, v, me = self.b, self.view, self.me
            for k, q, step in ((0, 0, 1), (1, 1, 3), (2, 1, 1), (3, 0, 3)):
                rc(b + k, v(me, q), v(me, q), at(self.axis, step)).start()

        def forward(self):
            b, v, me = self.b, self.view, self.me
            got(b, v(add(me, 3), 0))
            rc(b + 4, v(add(me, 3), 0), v(add(me, 3), 0), at(self.axis, 1)).start()
            got(b + 1, v(add(me, 1), 1))
            rc(b + 5, v(add(me, 1), 1), v(add(me, 1), 1), at(self.axis, 3)).start()

        def rest(self):
            got(self.b + 2, self.view(add(self.me, 3), 1))
            got(self.b + 3, self.view(add(self.me, 1), 0))
            got(self.b + 4, self.view(add(self.me, 2), 0))
            got(self.b + 5, self.view(add(self.me, 2), 1))

        def drain(self):
            for k in range(6):
                sent(self.b + k, self.view(self.me, 0))

    class Scatter:
        def __init__(self, axis, wide, narrow, recv, send):
            self.b, self.axis, self.wide, self.narrow, self.recv, self.send = take(6), axis, wide, narrow, recv, send
            self.me = x if axis == "x" else y

        def start(self):
            me = self.me
            for k, d, q, step in ((0, 2, 0, 1), (1, 2, 1, 3), (2, 1, 1, 1), (3, 3, 0, 3)):
                rc(self.b + k, self.narrow(add(me, d), q), self.recv(k), at(self.axis, step)).start()

        def forward(self):
            me = self.me
            for k, d, q, step in ((0, 1, 0, 1), (1, 3, 1, 3)):
                got(self.b + k, self.recv(k))
                part = self.wide(add(me, d), q)[...] + self.recv(k)[...].astype(F32)
                self.send(k)[...] = part.astype(self.send(k).dtype)
                rc(self.b + 4 + k, self.send(k), self.recv(4 + k), at(self.axis, step)).start()

        def result(self, q):
            i, k = (3, 4) if q == 0 else (2, 5)
            got(self.b + i, self.recv(i))
            got(self.b + k, self.recv(k))
            return self.wide(self.me, q)[...] + self.recv(i)[...].astype(F32) + self.recv(k)[...].astype(F32)

        def drain(self):
            for k in range(6):
                sent(self.b + k, self.recv(0))

    def gathers(c, h, one):
        if h == 0:
            return Gather("x", lambda p, q: one(y, p, q, c)), Gather("y", lambda p, q: one(p, slice(None), q, c))
        return Gather("y", lambda p, q: one(p, x, q, c)), Gather("x", lambda p, q: one(slice(None), p, q, c))

    def rows(q):
        return pl.ds(q * QR, QR)

    class Chunk:
        def __init__(self, j):
            self.w = CHUNKS[j] * 128
            self.o, self.ho = 256 * sum(CHUNKS[:j]), 128 * sum(CHUNKS[:j])
            self.red1, self.red2, self.gat = [], [], []
            hc = pl.ds(self.ho, self.w)
            for h in range(2):
                c = self.cols(h)
                pick = (lambda ref, d, q, c=c: ref.at[d, :, rows(q), c]) if h == 0 else (
                    lambda ref, d, q, c=c: ref.at[:, d, rows(q), c])
                self.red1.append(Scatter(
                    "yx"[h], lambda d, q, f=pick: f(p32, d, q), lambda d, q, f=pick: f(p16, d, q),
                    lambda k, h=h: r1.at[h, k, :, :, hc], lambda k, h=h: s1.at[h, k, :, :, hc]))
                part = lambda d, q, h=h: m32.at[h, d, rows(q), hc]
                self.red2.append(Scatter(
                    "xy"[h], part, part, lambda k, h=h: r2.at[h, k, :, hc], lambda k, h=h: s2.at[h, k, :, hc]))
                self.gat.append(gathers(c, h, lambda a, b, q, c: g_all.at[:, a, b, rows(q), c]))
            self.hc = hc

        def cols(self, h):
            return pl.ds(self.o + h * self.w, self.w)

        def product(self):
            def body(i, t):
                c = pl.ds(pl.multiple_of(self.o + i * 256, 256), 256)
                v = lax.dot_general(
                    go_all[...].reshape(512, DS), wd[c, :], NT, preferred_element_type=F32
                ).reshape(R, R, TB, 256)
                p32[:, :, :, c] = v
                p16[:, :, :, c] = v.astype(BF16)
                return t

            lax.fori_loop(0, self.w // 128, body, 0)

        def step(self, s):
            for h in range(2):
                if s == 0:
                    if h == 0:
                        self.product()
                    self.red1[h].start()
                if s == 1:
                    self.red1[h].forward()
                if s == 2:
                    for q in range(2):
                        m32[h, :, rows(q), self.hc] = self.red1[h].result(q)
                    self.red2[h].start()
                if s == 3:
                    self.red2[h].forward()
                if s == 4:
                    c = self.cols(h)
                    for q in range(2):
                        hg = self.red2[h].result(q)
                        gw, uw = gp[rows(q), c].astype(F32), up[rows(q), c].astype(F32)
                        sg = jax.nn.sigmoid(gw)
                        g_all[0, y, x, rows(q), c] = (hg * uw * sg * (1.0 + gw * (1.0 - sg))).astype(BF16)
                        g_all[1, y, x, rows(q), c] = (hg * (gw * sg)).astype(BF16)
                    self.gat[h][0].start()
                if s == 5:
                    self.gat[h][0].forward()
                if s == 6:
                    self.gat[h][0].rest()
                    self.gat[h][1].start()
                if s == 7:
                    self.gat[h][1].forward()
                if s == 8:
                    self.gat[h][1].rest()
            if s == 8:
                c = pl.ds(self.o, 2 * self.w)
                for a, w in ((0, wg), (1, wu)):
                    lhs = g_all[a, :, :, :, c].reshape(512, 2 * self.w)
                    acc[...] += lax.dot_general(
                        lhs, w[:, c], NT, preferred_element_type=F32).reshape(R, R, TB, DS)

        def drain(self):
            for h in range(2):
                for t in (self.red1[h], self.red2[h], *self.gat[h]):
                    t.drain()

    go_gather, inp_gather = RowGather(go_all), RowGather(inp_all)
    hid = [gathers(pl.ds(h * HALF, HALF), h, lambda a, b, q, c: hid_all.at[a, b, rows(q), c]) for h in range(2)]
    chunks = [Chunk(j) for j in range(len(CHUNKS))]
    rowsum = take(1)

    loads[0].wait()
    go_gather.start()
    loads[4].wait()
    inp_gather.start()

    loads[1].wait()
    loads[2].wait()
    gw, uw = gp[...].astype(F32), up[...].astype(F32)
    hid_all[y, x] = (gw * jax.nn.sigmoid(gw) * uw).astype(BF16)
    for f, s in hid:
        f.start()
    acc[...] = jnp.zeros_like(acc)
    go_gather.forward()
    go_gather.finish()
    for c in loads[3:4] + loads[5:]:
        c.wait()

    for t in range(9 + LAG * (len(CHUNKS) - 1)):
        for j, chunk in enumerate(chunks):
            if 0 <= t - LAG * j <= 8:
                chunk.step(t - LAG * j)
        if t == 0:
            inp_gather.forward()
        for f, s in hid:
            if t == HIDDEN[0]:
                f.forward()
            if t == HIDDEN[1]:
                f.rest()
                s.start()
            if t == HIDDEN[2]:
                s.forward()
            if t == HIDDEN[3]:
                s.rest()

    rc(rowsum, acc.at[:, pl.ds(2 * (1 - core), 2)], sib, other).start()
    inp_gather.finish()
    for f, s in hid:
        f.drain()
        s.drain()
    for chunk in chunks:
        chunk.drain()
    got(rowsum, sib)
    for i, ref in enumerate((own, to1, to2, to3)):
        p = add(z, i)
        ref[...] = (acc[p, pl.ds(2 * core, 2)] + sib[p]).reshape(RB, DS)
    sent(rowsum, sib)


WT = 512


def weights_kernel(inp_ref, go_ref, hid_ref, g_ref, dg_ref, du_ref, dd_ref, dg, du, dd, sem):
    inp, go = inp_ref[...].reshape(512, DS), go_ref[...].reshape(512, DS)

    def outs(i):
        c = pl.ds(pl.multiple_of(i * WT, WT), WT)
        k = lax.rem(i, 2)
        return (
            pltpu.make_async_copy(dg.at[k], dg_ref.at[:, c], sem.at[0, k]),
            pltpu.make_async_copy(du.at[k], du_ref.at[:, c], sem.at[1, k]),
            pltpu.make_async_copy(dd.at[k], dd_ref.at[c, :], sem.at[2, k]),
        )

    def body(i, t):
        c = pl.ds(pl.multiple_of(i * WT, WT), WT)
        k = lax.rem(i, 2)

        @pl.when(i >= 2)
        def _():
            for o in outs(i - 2):
                o.wait()

        a, b, d = outs(i)
        dg[k] = lax.dot_general(inp, g_ref[0, :, :, :, c].reshape(512, WT), TN, preferred_element_type=F32).astype(BF16)
        a.start()
        du[k] = lax.dot_general(inp, g_ref[1, :, :, :, c].reshape(512, WT), TN, preferred_element_type=F32).astype(BF16)
        b.start()
        dd[k] = lax.dot_general(hid_ref[:, :, :, c].reshape(512, WT), go, TN, preferred_element_type=F32).astype(BF16)
        d.start()
        return t

    n = FFS // WT
    lax.fori_loop(0, n, body, 0)
    for i in (n - 2, n - 1):
        for o in outs(i):
            o.wait()


def on_device(inputs, grad_out, gate_pre, up_pre, w_gate, w_up, w_down):
    anywhere = pl.BlockSpec(memory_space=pl.ANY)
    vmem = pl.BlockSpec(memory_space=pltpu.VMEM)
    tokens = pltpu.VMEM((2 * R, RB, DS), BF16)
    share = pltpu.VMEM((RB, DS), F32)
    nsem = 14 + 24 + 48 * len(CHUNKS) + 1
    hidden, grads, inp_all, go_all, own, to1, to2, to3 = pl.pallas_call(
        comm_kernel,
        out_shape=(
            pltpu.VMEM((R, R, TB, FFS), BF16), pltpu.VMEM((2, R, R, TB, FFS), BF16), tokens, tokens,
            share, share, share, share,
        ),
        in_specs=[anywhere] * 7,
        out_specs=[vmem] * 8,
        scratch_shapes=[
            pltpu.VMEM((TB, FFS), BF16),
            pltpu.VMEM((TB, FFS), BF16),
            pltpu.VMEM((DS, FFS), BF16),
            pltpu.VMEM((DS, FFS), BF16),
            pltpu.VMEM((FFS, DS), BF16),
            pltpu.VMEM((R, R, TB, FFS), F32),
            pltpu.VMEM((R, R, TB, FFS), BF16),
            pltpu.VMEM((2, 6, R, QR, HALF), BF16),
            pltpu.VMEM((2, 2, R, QR, HALF), BF16),
            pltpu.VMEM((2, R, TB, HALF), F32),
            pltpu.VMEM((2, 6, QR, HALF), T2),
            pltpu.VMEM((2, 2, QR, HALF), T2),
            pltpu.VMEM((R, R, TB, DS), F32),
            pltpu.VMEM((R, 2, TB, DS), F32),
            pltpu.SemaphoreType.DMA((7,)),
            pltpu.SemaphoreType.DMA((nsem,)),
            pltpu.SemaphoreType.DMA((nsem,)),
        ],
        compiler_params=pltpu.CompilerParams(
            collective_id=0, has_side_effects=True, vmem_limit_bytes=46 * 1024 * 1024
        ),
    )(inputs, grad_out, gate_pre, up_pre, w_gate, w_up, w_down)

    moved = [
        lax.ppermute(v, "row", [(d, (d + 2 * k) % (2 * R)) for d in range(2 * R)])
        for k, v in ((1, to1), (2, to2), (3, to3))
    ]
    grad_gate, grad_up, grad_down = pl.pallas_call(
        weights_kernel,
        out_shape=(
            jax.ShapeDtypeStruct((DS, FFS), BF16),
            jax.ShapeDtypeStruct((DS, FFS), BF16),
            jax.ShapeDtypeStruct((FFS, DS), BF16),
        ),
        in_specs=[vmem] * 4,
        out_specs=[anywhere] * 3,
        scratch_shapes=[
            pltpu.VMEM((2, DS, WT), BF16),
            pltpu.VMEM((2, DS, WT), BF16),
            pltpu.VMEM((2, WT, DS), BF16),
            pltpu.SemaphoreType.DMA((3, 2)),
        ],
        cost_estimate=pl.CostEstimate(flops=6 * 512 * DS * FFS, bytes_accessed=12 * DS * FFS, transcendentals=0),
        compiler_params=pltpu.CompilerParams(vmem_limit_bytes=32 * 1024 * 1024),
    )(inp_all, go_all, hidden, grads)
    grad_inputs = (own + moved[0] + moved[1] + moved[2]).astype(BF16)
    return (grad_inputs, grad_gate, grad_up, grad_down)


def solution(mesh):
    placed = (
        P("row", "col"),
        P("row", "col"),
        P("col", "row"),
        P("col", "row"),
        P("col", "row"),
        P("col", "row"),
        P("row", "col"),
    )
    return jax.shard_map(
        on_device,
        mesh=mesh,
        in_specs=placed,
        out_specs=(P("row", "col"), P("col", "row"), P("col", "row"), P("row", "col")),
        check_vma=False,
    )
```

time: 310 us -> 116 us (0.37)
  waiting for transfers between devices: 210 us -> 0.01 us
  Pallas kernels: 0 us -> 111 us
  matrix products: 36.5 us -> 0 us
  blocking collectives: 30.5 us -> 0 us
  between operations: 13.8 us -> 0.68 us
  local copies, waits for them, and re-layouts: 11.9 us -> 0 us
  starting transfers between devices: 0.2 us -> 3.77 us
    pallas_call x0 -> x2, Pallas kernels: none -> 111 us  [the longest x1 103 us: on_device(): pl.pallas_call(comm_kernel, out_shape=(pltpu.VMEM((R, R, TB, FFS), BF16),...]
    reduce_scatter x2 -> x0, waiting for transfers between devices: 107 us -> none  [the longest x1 82.3 us: on_device(): lax.psum_scatter(lax.dot_general(grad_out_all, w_down, last_last, preferr...]
    all_gather x3 -> x0, waiting for transfers between devices: 102 us -> none  [the longest x1 49.2 us: on_device(): lax.all_gather(gate_grad, 'col', axis=0, tiled=True)]
    dot_general x6 -> x0, matrix products: 36.5 us -> none  [the longest x1 7.08 us: on_device(): lax.dot_general(grad_out_all, w_down, last_last, preferred_element_type=j...]
    all_gather x2 -> x0, blocking collectives: 30.5 us -> none  [the longest x1 15.9 us: on_device(): lax.all_gather(grad_out, 'row', axis=0, tiled=True)]
    unnamed x8 -> x0, local copies, waits for them, and re-layouts: 11.9 us -> none
    ppermute x0 -> x3, starting transfers between devices: none -> 3.77 us  [on_device(): lax.ppermute(v, 'row', [(d, (d + 2 * k) % (2 * R)) for d in range(2 * R)])]
  transfers between devices with their start and end apart: 5 -> 3, of which waited for: 5 -> 0; matrix products, arithmetic and copies ran while one was open for 13% -> 0% of each run, Pallas kernels for 0% -> 7%
where the time goes in v2:
time: 116 us
  Pallas kernels  111 us (96%)
  starting transfers between devices  3.77 us (3%)
    pallas_call x1, Pallas kernels, on_device(): pl.pallas_call(comm_kernel, out_shape=(pltpu.VMEM((R, R, TB, FFS), BF16),...  103 us
    pallas_call x1, Pallas kernels, on_device(): pl.pallas_call(weights_kernel, out_shape=(jax.ShapeDtypeStruct((DS, FFS),...  8.1 us
    ppermute x3, starting transfers between devices, on_device(): lax.ppermute(v, 'row', [(d, (d + 2 * k) % (2 * R)) for d in range(2 * R)])  3.77 us
  transfers between devices with their start and end apart: 3, of which 0 were waited for; matrix products, arithmetic and copies ran while one was open for 0% of the time, Pallas kernels for 7%

profile of v2, /device:TPU:1, one launch (start us, length us, event | category | flops | bytes accessed | tf_op | source)
XLA Modules:
  0.0 116.0 jit_solution(4776892560848831761)
XLA Ops:
  0.6 102.8 %shard_map.102 = (bf16[4,4,32,3584]{3,2,1,0:T(8,128)(2,1)S(1)}, bf16[2,4,4,32,3584]{4,3,2,1,0:T(8,128)(2,1)S(1)}, bf16[8,64,512]{2,1,0:T(8,128)(2,1)S(1)}, bf16[...) custom-call(bf16[64,512]{1,0:T(8,128)(2,1)} %inp_ref.1, ...), custom_call_target="tpu_custom_call" | custom-call | tf_op jit(solution)/shard_map/pallas_call | solution.py:342
  103.4 0.1 collective-permute-start
  103.5 2.5 %collective-permute-start.1 = (f32[64,512]{1,0:T(8,128)S(1)}, f32[64,512]{1,0:T(8,128)S(1)}, u32[]{:S(2)}, u32[]{:S(2)}) collective-permute-start(f32[64,512]{1,0:T(8,128)S(1)} %get-tuple-element.17), channel_id=1, source_target_pairs={{0,64},{16,80},{32,96},{48,112},{64,0},{80,16},{96,32},{112,48},{1... | collective-permute-start | bytes 393224 | tf_op jit(solution)/shard_map/ppermute | solution.py:375
  106.0 1.2 %collective-permute-start.2 = (f32[64,512]{1,0:T(8,128)S(1)}, f32[64,512]{1,0:T(8,128)S(1)}, u32[]{:S(2)}, u32[]{:S(2)}) collective-permute-start(f32[64,512]{1,0:T(8,128)S(1)} %get-tuple-element.18), channel_id=1, source_target_pairs={{0,96},{16,112},{32,0},{48,16},{64,32},{80,48},{96,64},{112,80},{1... | collective-permute-start | bytes 393224 | tf_op jit(solution)/shard_map/ppermute | solution.py:375
  107.2 8.1 %shard_map.103 = (bf16[512,3584]{1,0:T(8,128)(2,1)}, bf16[512,3584]{1,0:T(8,128)(2,1)}, bf16[3584,512]{1,0:T(8,128)(2,1)}) custom-call(bf16[8,64,512]{2,1,0:T(8,128)(2,1)S(1)} %get-tuple-element.19.inp_ref, bf16[8,64,512]{2,1,0:T(8,128)(2,1)S(1)} %get-tuple-element.20.go_ref, bf16[4,4,32,3584]{3,2,1,0:T(8,128)(2,1)S(1)} %get-tuple-element.21.hid_ref, ...), custom_call_target="tpu_custom_call" | custom-call | flops 5637144576 | bytes 22020096 | tf_op jit(solution)/shard_map/pallas_call | solution.py:378
  115.3 0.0 collective-permute-done
  115.3 0.0 collective-permute-done.1
  115.3 0.0 collective-permute-done.2
  115.3 0.7 add_convert_fusion
Async XLA Ops:
  103.4 11.9 %collective-permute-start = (f32[64,512]{1,0:T(8,128)S(1)}, f32[64,512]{1,0:T(8,128)S(1)}, u32[]{:S(2)}, u32[]{:S(2)}) collective-permute-start(f32[64,512]{1,0:T(8,128)S(1)} %get-tuple-element.16), channel_id=1, source_target_pairs={{0,32},{16,48},{32,64},{48,80},{64,96},{80,112},{96,0},{112,16},{1... | collective-permute-start | bytes 393224 | tf_op jit(solution)/shard_map/ppermute | solution.py:375
  103.5 11.8 %collective-permute-start.1 = (f32[64,512]{1,0:T(8,128)S(1)}, f32[64,512]{1,0:T(8,128)S(1)}, u32[]{:S(2)}, u32[]{:S(2)}) collective-permute-start(f32[64,512]{1,0:T(8,128)S(1)} %get-tuple-element.17), channel_id=1, source_target_pairs={{0,64},{16,80},{32,96},{48,112},{64,0},{80,16},{96,32},{112,48},{1... | collective-permute-start | bytes 393224 | tf_op jit(solution)/shard_map/ppermute | solution.py:375
  106.0 9.3 %collective-permute-start.2 = (f32[64,512]{1,0:T(8,128)S(1)}, f32[64,512]{1,0:T(8,128)S(1)}, u32[]{:S(2)}, u32[]{:S(2)}) collective-permute-start(f32[64,512]{1,0:T(8,128)S(1)} %get-tuple-element.18), channel_id=1, source_target_pairs={{0,96},{16,112},{32,0},{48,16},{64,32},{80,48},{96,64},{112,80},{1... | collective-permute-start | bytes 393224 | tf_op jit(solution)/shard_map/ppermute | solution.py:375

commit v3 on v2

--- a/solution.py
+++ b/solution.py
@@ -16,19 +16,18 @@
 QR = TB // 2
 DS = 512
 RB = 64
-T2 = F32
-
-
-CHUNKS = (4, 4, 3, 3)
+
+
+CHUNKS = (4, 4, 4, 2)
+FAR = 2
 LAG = 1
-HIDDEN = (0, 1, 4, 7)
 
 
 def comm_kernel(
     inp_ref, go_ref, gp_ref, up_ref, wg_ref, wu_ref, wd_ref,
-    hid_all, g_all, inp_all, go_all, own, to1, to2, to3,
+    hid_all, g_all, inp_all, go_all, gi,
     gp, up, wg, wu, wd,
-    p32, p16, r1, s1, m32, r2, s2, acc, sib,
+    p32, p16, r1, s1, m32, m16, r2, s2, acc, sib, zout, zin,
     loc, ss, rs,
 ):
     col, row = lax.axis_index("col"), lax.axis_index("row")
@@ -116,9 +115,11 @@
             got(b + 1, v(add(me, 1), 1))
             rc(b + 5, v(add(me, 1), 1), v(add(me, 1), 1), at(self.axis, 3)).start()
 
-        def rest(self):
+        def near(self):
             got(self.b + 2, self.view(add(self.me, 3), 1))
             got(self.b + 3, self.view(add(self.me, 1), 0))
+
+        def far(self):
             got(self.b + 4, self.view(add(self.me, 2), 0))
             got(self.b + 5, self.view(add(self.me, 2), 1))
 
@@ -175,9 +176,9 @@
                 self.red1.append(Scatter(
                     "yx"[h], lambda d, q, f=pick: f(p32, d, q), lambda d, q, f=pick: f(p16, d, q),
                     lambda k, h=h: r1.at[h, k, :, :, hc], lambda k, h=h: s1.at[h, k, :, :, hc]))
-                part = lambda d, q, h=h: m32.at[h, d, rows(q), hc]
                 self.red2.append(Scatter(
-                    "xy"[h], part, part, lambda k, h=h: r2.at[h, k, :, hc], lambda k, h=h: s2.at[h, k, :, hc]))
+                    "xy"[h], lambda d, q, h=h: m32.at[h, d, rows(q), hc], lambda d, q, h=h: m16.at[h, d, rows(q), hc],
+                    lambda k, h=h: r2.at[h, k, :, hc], lambda k, h=h: s2.at[h, k, :, hc]))
                 self.gat.append(gathers(c, h, lambda a, b, q, c: g_all.at[:, a, b, rows(q), c]))
             self.hc = hc
 
@@ -206,7 +207,9 @@
                     self.red1[h].forward()
                 if s == 2:
                     for q in range(2):
-                        m32[h, :, rows(q), self.hc] = self.red1[h].result(q)
+                        v = self.red1[h].result(q)
+                        m32[h, :, rows(q), self.hc] = v
+                        m16[h, :, rows(q), self.hc] = v.astype(BF16)
                     self.red2[h].start()
                 if s == 3:
                     self.red2[h].forward()
@@ -222,13 +225,15 @@
                 if s == 5:
                     self.gat[h][0].forward()
                 if s == 6:
-                    self.gat[h][0].rest()
+                    self.gat[h][0].near()
+                    self.gat[h][0].far()
                     self.gat[h][1].start()
                 if s == 7:
                     self.gat[h][1].forward()
                 if s == 8:
-                    self.gat[h][1].rest()
-            if s == 8:
+                    self.gat[h][1].near()
+                    self.gat[h][1].far()
+            if s == 9:
                 c = pl.ds(self.o, 2 * self.w)
                 for a, w in ((0, wg), (1, wu)):
                     lhs = g_all[a, :, :, :, c].reshape(512, 2 * self.w)
@@ -241,9 +246,17 @@
                     t.drain()
 
     go_gather, inp_gather = RowGather(go_all), RowGather(inp_all)
-    hid = [gathers(pl.ds(h * HALF, HALF), h, lambda a, b, q, c: hid_all.at[a, b, rows(q), c]) for h in range(2)]
+    hid = []
+    for h in range(2):
+        view = lambda a, b, q, h=h: hid_all.at[a, b, rows(q), pl.ds(h * HALF, HALF)]
+        if h == 0:
+            hid.append((Gather("x", lambda p, q, v=view: v(y, p, q)), [
+                Gather("y", lambda p, q, v=view, k=k: v(p, add(x, k), q)) for k in range(R)]))
+        else:
+            hid.append((Gather("y", lambda p, q, v=view: v(p, x, q)), [
+                Gather("x", lambda p, q, v=view, k=k: v(add(y, k), p, q)) for k in range(R)]))
     chunks = [Chunk(j) for j in range(len(CHUNKS))]
-    rowsum = take(1)
+    rowsum = take(4)
 
     loads[0].wait()
     go_gather.start()
@@ -256,47 +269,69 @@
     hid_all[y, x] = (gw * jax.nn.sigmoid(gw) * uw).astype(BF16)
     for f, s in hid:
         f.start()
+        s[0].start()
     acc[...] = jnp.zeros_like(acc)
+    for f, s in hid:
+        f.forward()
+        f.near()
+        s[1].start()
+        s[3].start()
     go_gather.forward()
     go_gather.finish()
     for c in loads[3:4] + loads[5:]:
         c.wait()
 
-    for t in range(9 + LAG * (len(CHUNKS) - 1)):
+    last = 8 + LAG * (len(CHUNKS) - 1)
+    for t in range(last + 1):
         for j, chunk in enumerate(chunks):
             if 0 <= t - LAG * j <= 8:
                 chunk.step(t - LAG * j)
+            if t - LAG * j == 8 and t < last:
+                chunk.step(9)
         if t == 0:
             inp_gather.forward()
         for f, s in hid:
-            if t == HIDDEN[0]:
-                f.forward()
-            if t == HIDDEN[1]:
-                f.rest()
-                s.start()
-            if t == HIDDEN[2]:
-                s.forward()
-            if t == HIDDEN[3]:
-                s.rest()
+            if t == last - FAR:
+                f.far()
+                s[2].start()
+            if t == last - 1:
+                for k in (0, 1, 3):
+                    s[k].forward()
+            if t == last:
+                s[2].forward()
+    chunks[-1].step(9)
 
     rc(rowsum, acc.at[:, pl.ds(2 * (1 - core), 2)], sib, other).start()
     inp_gather.finish()
-    for f, s in hid:
-        f.drain()
-        s.drain()
     for chunk in chunks:
         chunk.drain()
     got(rowsum, sib)
-    for i, ref in enumerate((own, to1, to2, to3)):
-        p = add(z, i)
-        ref[...] = (acc[p, pl.ds(2 * core, 2)] + sib[p]).reshape(RB, DS)
+    for i in range(3):
+        p = add(z, i + 1)
+        zout[i] = (acc[p, pl.ds(2 * core, 2)] + sib[p]).reshape(RB, DS).astype(BF16)
+        rc(rowsum + 1 + i, zout.at[i], zin.at[i], zdev[i]).start()
+    total = (acc[z, pl.ds(2 * core, 2)] + sib[z]).reshape(RB, DS)
+    for f, s in hid:
+        for g in s:
+            g.near()
+            g.far()
+        for g in [f] + s:
+            g.drain()
+    for i in range(3):
+        got(rowsum + 1 + i, zin.at[i])
+        total = total + zin[i].astype(F32)
+    gi[...] = total.astype(BF16)
     sent(rowsum, sib)
+    for i in range(3):
+        sent(rowsum + 1 + i, zout.at[i])
 
 
 WT = 512
 
 
-def weights_kernel(inp_ref, go_ref, hid_ref, g_ref, dg_ref, du_ref, dd_ref, dg, du, dd, sem):
+def weights_kernel(inp_ref, go_ref, hid_ref, g_ref, gi_ref, gi_out, dg_ref, du_ref, dd_ref, dg, du, dd, sem, one):
+    save = pltpu.make_async_copy(gi_ref, gi_out, one)
+    save.start()
     inp, go = inp_ref[...].reshape(512, DS), go_ref[...].reshape(512, DS)
 
     def outs(i):
@@ -331,22 +366,22 @@
     for i in (n - 2, n - 1):
         for o in outs(i):
             o.wait()
+    save.wait()
 
 
 def on_device(inputs, grad_out, gate_pre, up_pre, w_gate, w_up, w_down):
     anywhere = pl.BlockSpec(memory_space=pl.ANY)
     vmem = pl.BlockSpec(memory_space=pltpu.VMEM)
     tokens = pltpu.VMEM((2 * R, RB, DS), BF16)
-    share = pltpu.VMEM((RB, DS), F32)
-    nsem = 14 + 24 + 48 * len(CHUNKS) + 1
-    hidden, grads, inp_all, go_all, own, to1, to2, to3 = pl.pallas_call(
+    nsem = 14 + 60 + 48 * len(CHUNKS) + 4
+    hidden, grads, inp_all, go_all, gi = pl.pallas_call(
         comm_kernel,
         out_shape=(
             pltpu.VMEM((R, R, TB, FFS), BF16), pltpu.VMEM((2, R, R, TB, FFS), BF16), tokens, tokens,
-            share, share, share, share,
+            pltpu.VMEM((RB, DS), BF16),
         ),
         in_specs=[anywhere] * 7,
-        out_specs=[vmem] * 8,
+        out_specs=[vmem] * 5,
         scratch_shapes=[
             pltpu.VMEM((TB, FFS), BF16),
             pltpu.VMEM((TB, FFS), BF16),
@@ -358,10 +393,13 @@
             pltpu.VMEM((2, 6, R, QR, HALF), BF16),
             pltpu.VMEM((2, 2, R, QR, HALF), BF16),
             pltpu.VMEM((2, R, TB, HALF), F32),
-            pltpu.VMEM((2, 6, QR, HALF), T2),
-            pltpu.VMEM((2, 2, QR, HALF), T2),
+            pltpu.VMEM((2, R, TB, HALF), BF16),
+            pltpu.VMEM((2, 6, QR, HALF), BF16),
+            pltpu.VMEM((2, 2, QR, HALF), BF16),
             pltpu.VMEM((R, R, TB, DS), F32),
             pltpu.VMEM((R, 2, TB, DS), F32),
+            pltpu.VMEM((3, RB, DS), BF16),
+            pltpu.VMEM((3, RB, DS), BF16),
             pltpu.SemaphoreType.DMA((7,)),
             pltpu.SemaphoreType.DMA((nsem,)),
             pltpu.SemaphoreType.DMA((nsem,)),
@@ -371,30 +409,26 @@
         ),
     )(inputs, grad_out, gate_pre, up_pre, w_gate, w_up, w_down)
 
-    moved = [
-        lax.ppermute(v, "row", [(d, (d + 2 * k) % (2 * R)) for d in range(2 * R)])
-        for k, v in ((1, to1), (2, to2), (3, to3))
-    ]
-    grad_gate, grad_up, grad_down = pl.pallas_call(
+    return pl.pallas_call(
         weights_kernel,
         out_shape=(
+            jax.ShapeDtypeStruct((RB, DS), BF16),
             jax.ShapeDtypeStruct((DS, FFS), BF16),
             jax.ShapeDtypeStruct((DS, FFS), BF16),
             jax.ShapeDtypeStruct((FFS, DS), BF16),
         ),
-        in_specs=[vmem] * 4,
-        out_specs=[anywhere] * 3,
+        in_specs=[vmem] * 5,
+        out_specs=[anywhere] * 4,
         scratch_shapes=[
             pltpu.VMEM((2, DS, WT), BF16),
             pltpu.VMEM((2, DS, WT), BF16),
             pltpu.VMEM((2, WT, DS), BF16),
             pltpu.SemaphoreType.DMA((3, 2)),
+            pltpu.SemaphoreType.DMA,
         ],
         cost_estimate=pl.CostEstimate(flops=6 * 512 * DS * FFS, bytes_accessed=12 * DS * FFS, transcendentals=0),
         compiler_params=pltpu.CompilerParams(vmem_limit_bytes=32 * 1024 * 1024),
-    )(inp_all, go_all, hidden, grads)
-    grad_inputs = (own + moved[0] + moved[1] + moved[2]).astype(BF16)
-    return (grad_inputs, grad_gate, grad_up, grad_down)
+    )(inp_all, go_all, hidden, grads, gi)
 
 
 def solution(mesh):

time: 116 us -> 105 us (0.905)
  Pallas kernels: 111 us -> 104 us
  starting transfers between devices: 3.77 us -> 0 us
    pallas_call x1, Pallas kernels: 103 us -> 96.2 us  [on_device(): pl.pallas_call(comm_kernel, out_shape=(pltpu.VMEM((R, R, TB, FFS), BF16),...]
    ppermute x3 -> x0, starting transfers between devices: 3.77 us -> none  [on_device(): lax.ppermute(v, 'row', [(d, (d + 2 * k) % (2 * R)) for d in range(2 * R)])]
  transfers between devices with their start and end apart: 3 -> 0, of which waited for: 0 -> 0; matrix products, arithmetic and copies ran while one was open for 0% -> 0% of each run, Pallas kernels for 7% -> 0%
where the time goes in v3:
time: 105 us
  Pallas kernels  104 us (99%)
    pallas_call x1, Pallas kernels, on_device(): pl.pallas_call(comm_kernel, out_shape=(pltpu.VMEM((R, R, TB, FFS), BF16),...  96.2 us
    pallas_call x1, Pallas kernels, on_device(): pl.pallas_call(weights_kernel, out_shape=(jax.ShapeDtypeStruct((RB, DS),...  8.12 us

profile of v3, /device:TPU:1, one launch (start us, length us, event | category | flops | bytes accessed | tf_op | source)
XLA Modules:
  0.0 104.9 jit_solution(10441276556388599283)
XLA Ops:
  0.6 96.2 %shard_map.102 = (bf16[4,4,32,3584]{3,2,1,0:T(8,128)(2,1)S(1)}, bf16[2,4,4,32,3584]{4,3,2,1,0:T(8,128)(2,1)S(1)}, bf16[8,64,512]{2,1,0:T(8,128)(2,1)S(1)}, bf16[...) custom-call(bf16[64,512]{1,0:T(8,128)(2,1)} %inp_ref.1, bf16[64,512]{1,0:T(8,128)(2,1)} %go_ref.1, bf16[32,3584]{1,0:T(8,128)(2,1)} %gp_ref.1, ...), custom_call_target="tpu_custom_call" | custom-call | tf_op jit(solution)/shard_map/pallas_call | solution.py:377
  96.8 8.1 %shard_map.103 = (bf16[64,512]{1,0:T(8,128)(2,1)}, bf16[512,3584]{1,0:T(8,128)(2,1)}, bf16[512,3584]{1,0:T(8,128)(2,1)}, bf16[3584,512]{1,0:T(8,128)(2,1)}) custom-call(bf16[8,64,512]{2,1,0:T(8,128)(2,1)S(1)} %get-tuple-element.9.inp_ref, bf16[8,64,512]{2,1,0:T(8,128)(2,1)S(1)} %get-tuple-element.10.go_ref, ...), custom_call_target="tpu_custom_call" | custom-call | flops 5637144576 | bytes 22020096 | tf_op jit(solution)/shard_map/pallas_call | solution.py:412

commit v4 on v3

--- a/solution.py
+++ b/solution.py
@@ -25,8 +25,8 @@
 
 def comm_kernel(
     inp_ref, go_ref, gp_ref, up_ref, wg_ref, wu_ref, wd_ref,
-    hid_all, g_all, inp_all, go_all, gi,
-    gp, up, wg, wu, wd,
+    dg, du, dd, gi,
+    hid_all, g_all, inp_all, inp_t, go_all, gp, up, wg, wu, wd,
     p32, p16, r1, s1, m32, m16, r2, s2, acc, sib, zout, zin,
     loc, ss, rs,
 ):
@@ -240,6 +240,16 @@
                     acc[...] += lax.dot_general(
                         lhs, w[:, c], NT, preferred_element_type=F32).reshape(R, R, TB, DS)
 
+        def weights(self):
+            def body(i, t):
+                c = pl.ds(pl.multiple_of(self.o + i * 256, 256), 256)
+                for a, d in ((0, dg), (1, du)):
+                    v = g_all[a, :, :, :, c].reshape(512, 256)
+                    d[:, c] = jnp.dot(inp_t[...], v, preferred_element_type=F32).astype(BF16)
+                return t
+
+            lax.fori_loop(0, self.w // 128, body, 0)
+
         def drain(self):
             for h in range(2):
                 for t in (self.red1[h], self.red2[h], *self.gat[h]):
@@ -286,10 +296,11 @@
         for j, chunk in enumerate(chunks):
             if 0 <= t - LAG * j <= 8:
                 chunk.step(t - LAG * j)
-            if t - LAG * j == 8 and t < last:
-                chunk.step(9)
         if t == 0:
             inp_gather.forward()
+        if t == 4:
+            inp_gather.finish()
+            inp_t[...] = inp_all[...].reshape(512, DS).T
         for f, s in hid:
             if t == last - FAR:
                 f.far()
@@ -299,12 +310,14 @@
                     s[k].forward()
             if t == last:
                 s[2].forward()
-    chunks[-1].step(9)
+        for j, chunk in enumerate(chunks):
+            if t - LAG * j == 8:
+                chunk.step(9)
+                if t < last:
+                    chunk.weights()
 
     rc(rowsum, acc.at[:, pl.ds(2 * (1 - core), 2)], sib, other).start()
-    inp_gather.finish()
-    for chunk in chunks:
-        chunk.drain()
+    chunks[-1].weights()
     got(rowsum, sib)
     for i in range(3):
         p = add(z, i + 1)
@@ -315,8 +328,19 @@
         for g in s:
             g.near()
             g.far()
+
+    def down(i, t):
+        c = pl.ds(pl.multiple_of(i * 512, 512), 512)
+        v = hid_all[:, :, :, c].reshape(512, 512)
+        dd[c, :] = lax.dot_general(v, go_all[...].reshape(512, DS), TN, preferred_element_type=F32).astype(BF16)
+        return t
+
+    lax.fori_loop(0, FFS // 512, down, 0)
+    for f, s in hid:
         for g in [f] + s:
             g.drain()
+    for chunk in chunks:
+        chunk.drain()
     for i in range(3):
         got(rowsum + 1 + i, zin.at[i])
         total = total + zin[i].astype(F32)
@@ -326,63 +350,31 @@
         sent(rowsum + 1 + i, zout.at[i])
 
 
-WT = 512
-
-
-def weights_kernel(inp_ref, go_ref, hid_ref, g_ref, gi_ref, gi_out, dg_ref, du_ref, dd_ref, dg, du, dd, sem, one):
-    save = pltpu.make_async_copy(gi_ref, gi_out, one)
-    save.start()
-    inp, go = inp_ref[...].reshape(512, DS), go_ref[...].reshape(512, DS)
-
-    def outs(i):
-        c = pl.ds(pl.multiple_of(i * WT, WT), WT)
-        k = lax.rem(i, 2)
-        return (
-            pltpu.make_async_copy(dg.at[k], dg_ref.at[:, c], sem.at[0, k]),
-            pltpu.make_async_copy(du.at[k], du_ref.at[:, c], sem.at[1, k]),
-            pltpu.make_async_copy(dd.at[k], dd_ref.at[c, :], sem.at[2, k]),
-        )
-
-    def body(i, t):
-        c = pl.ds(pl.multiple_of(i * WT, WT), WT)
-        k = lax.rem(i, 2)
-
-        @pl.when(i >= 2)
-        def _():
-            for o in outs(i - 2):
-                o.wait()
-
-        a, b, d = outs(i)
-        dg[k] = lax.dot_general(inp, g_ref[0, :, :, :, c].reshape(512, WT), TN, preferred_element_type=F32).astype(BF16)
-        a.start()
-        du[k] = lax.dot_general(inp, g_ref[1, :, :, :, c].reshape(512, WT), TN, preferred_element_type=F32).astype(BF16)
-        b.start()
-        dd[k] = lax.dot_general(hid_ref[:, :, :, c].reshape(512, WT), go, TN, preferred_element_type=F32).astype(BF16)
-        d.start()
-        return t
-
-    n = FFS // WT
-    lax.fori_loop(0, n, body, 0)
-    for i in (n - 2, n - 1):
-        for o in outs(i):
-            o.wait()
-    save.wait()
+def store_kernel(dg, du, dd, gi, dg_ref, du_ref, dd_ref, gi_ref, sem):
+    pairs = ((dg, dg_ref), (du, du_ref), (dd, dd_ref), (gi, gi_ref))
+    copies = [pltpu.make_async_copy(a, b, sem.at[i]) for i, (a, b) in enumerate(pairs)]
+    for c in copies:
+        c.start()
+    for c in copies:
+        c.wait()
 
 
 def on_device(inputs, grad_out, gate_pre, up_pre, w_gate, w_up, w_down):
     anywhere = pl.BlockSpec(memory_space=pl.ANY)
     vmem = pl.BlockSpec(memory_space=pltpu.VMEM)
-    tokens = pltpu.VMEM((2 * R, RB, DS), BF16)
+    shapes = ((DS, FFS), (DS, FFS), (FFS, DS), (RB, DS))
     nsem = 14 + 60 + 48 * len(CHUNKS) + 4
-    hidden, grads, inp_all, go_all, gi = pl.pallas_call(
+    dg, du, dd, gi = pl.pallas_call(
         comm_kernel,
-        out_shape=(
-            pltpu.VMEM((R, R, TB, FFS), BF16), pltpu.VMEM((2, R, R, TB, FFS), BF16), tokens, tokens,
-            pltpu.VMEM((RB, DS), BF16),
-        ),
+        out_shape=[pltpu.VMEM(v, BF16) for v in shapes],
         in_specs=[anywhere] * 7,
-        out_specs=[vmem] * 5,
+        out_specs=[vmem] * 4,
         scratch_shapes=[
+            pltpu.VMEM((R, R, TB, FFS), BF16),
+            pltpu.VMEM((2, R, R, TB, FFS), BF16),
+            pltpu.VMEM((2 * R, RB, DS), BF16),
+            pltpu.VMEM((DS, 512), BF16),
+            pltpu.VMEM((2 * R, RB, DS), BF16),
             pltpu.VMEM((TB, FFS), BF16),
             pltpu.VMEM((TB, FFS), BF16),
             pltpu.VMEM((DS, FFS), BF16),
@@ -405,30 +397,19 @@
             pltpu.SemaphoreType.DMA((nsem,)),
         ],
         compiler_params=pltpu.CompilerParams(
-            collective_id=0, has_side_effects=True, vmem_limit_bytes=46 * 1024 * 1024
+            collective_id=0, has_side_effects=True, vmem_limit_bytes=50 * 1024 * 1024
         ),
     )(inputs, grad_out, gate_pre, up_pre, w_gate, w_up, w_down)
 
-    return pl.pallas_call(
-        weights_kernel,
-        out_shape=(
-            jax.ShapeDtypeStruct((RB, DS), BF16),
-            jax.ShapeDtypeStruct((DS, FFS), BF16),
-            jax.ShapeDtypeStruct((DS, FFS), BF16),
-            jax.ShapeDtypeStruct((FFS, DS), BF16),
-        ),
-        in_specs=[vmem] * 5,
+    dg, du, dd, gi = pl.pallas_call(
+        store_kernel,
+        out_shape=[jax.ShapeDtypeStruct(v, BF16) for v in shapes],
+        in_specs=[vmem] * 4,
         out_specs=[anywhere] * 4,
-        scratch_shapes=[
-            pltpu.VMEM((2, DS, WT), BF16),
-            pltpu.VMEM((2, DS, WT), BF16),
-            pltpu.VMEM((2, WT, DS), BF16),
-            pltpu.SemaphoreType.DMA((3, 2)),
-            pltpu.SemaphoreType.DMA,
-        ],
-        cost_estimate=pl.CostEstimate(flops=6 * 512 * DS * FFS, bytes_accessed=12 * DS * FFS, transcendentals=0),
-        compiler_params=pltpu.CompilerParams(vmem_limit_bytes=32 * 1024 * 1024),
-    )(inp_all, go_all, hidden, grads, gi)
+        scratch_shapes=[pltpu.SemaphoreType.DMA((4,))],
+        compiler_params=pltpu.CompilerParams(vmem_limit_bytes=4 * 1024 * 1024),
+    )(dg, du, dd, gi)
+    return (gi, dg, du, dd)
 
 
 def solution(mesh):

time: 105 us -> 102 us (0.971)
  Pallas kernels: 104 us -> 101 us
    pallas_call x2, Pallas kernels: 104 us -> 101 us  [the longest x1 96.7 us: on_device(): pl.pallas_call(comm_kernel, out_shape=[pltpu.VMEM(v, BF16) for v in shape...]
where the time goes in v4:
time: 102 us
  Pallas kernels  101 us (99%)
    pallas_call x1, Pallas kernels, on_device(): pl.pallas_call(comm_kernel, out_shape=[pltpu.VMEM(v, BF16) for v in shape...  96.7 us
    pallas_call x1, Pallas kernels, on_device(): pl.pallas_call(store_kernel, out_shape=[jax.ShapeDtypeStruct(v, BF16) for...  4.29 us

profile of v4, /device:TPU:1, one launch (start us, length us, event | category | flops | bytes accessed | tf_op | source)
XLA Modules:
  0.0 101.7 jit_solution(8701263878109500801)
XLA Ops:
  0.6 96.7 %shard_map.102 = (bf16[512,3584]{1,0:T(8,128)(2,1)S(1)}, bf16[512,3584]{1,0:T(8,128)(2,1)S(1)}, bf16[3584,512]{1,0:T(8,128)(2,1)S(1)}, bf16[64,512]{1,0:T(8,128)(2,1)S(1)}) custom-call(bf16[64,512]{1,0:T(8,128)(2,1)} %inp_ref.1, bf16[64,512]{1,0:T(8,128)(2,1)} %go_ref.1, bf16[32,3584]{1,0:T(8,128)(2,1)} %gp_ref.1, bf16[32,3584]{1,0:T(8,128)(2,1)} %up_ref.1, ...), custom_call_target="tpu_custom_call" | custom-call | tf_op jit(solution)/shard_map/pallas_call | solution.py:367
  97.4 4.3 %shard_map.103 = (bf16[512,3584]{1,0:T(8,128)(2,1)}, bf16[512,3584]{1,0:T(8,128)(2,1)}, bf16[3584,512]{1,0:T(8,128)(2,1)}, bf16[64,512]{1,0:T(8,128)(2,1)}) custom-call(bf16[512,3584]{1,0:T(8,128)(2,1)S(1)} %get-tuple-element.12.dg, bf16[512,3584]{1,0:T(8,128)(2,1)S(1)} %get-tuple-element.13.du, bf16[3584,512]{1,0:T(8,128)(2,1)S(1)} %get-tuple-element.14.dd, ...), custom_call_target="tpu_custom_call" | custom-call | tf_op jit(solution)/shard_map/pallas_call | solution.py:404

commit v5 on v4

--- a/solution.py
+++ b/solution.py
@@ -19,8 +19,11 @@
 
 
 CHUNKS = (4, 4, 4, 2)
-FAR = 2
-LAG = 1
+LAG_SUM = 0.6
+LAG_GATHER = 0.6
+NEAR = -1
+FAR = 0.4
+AHEAD = 1.0
 
 
 def comm_kernel(
@@ -47,6 +50,7 @@
 
     zdev = [{"row": add(z, k) * 2 + core} for k in (1, 2, 3)]
     other = {"row": z * 2 + 1 - core}
+    zfar = [[{"row": add(z, k) * 2 + lax.rem(core + j, 2)} for j in range(2)] for k in (1, 2, 3)]
 
     def rc(k, src, dst, dev):
         return pltpu.make_async_remote_copy(
@@ -70,7 +74,7 @@
         c.start()
 
     barrier = pltpu.get_barrier_semaphore()
-    peers = [at("x", 1), at("x", 3), at("y", 1), at("y", 3), other] + zdev
+    peers = [at("x", 1), at("x", 3), at("y", 1), at("y", 3), other] + sum(zfar, [])
     for d in peers:
         pl.semaphore_signal(barrier, inc=1, device_id=d, device_id_type=MESH)
     pl.semaphore_wait(barrier, len(peers))
@@ -266,7 +270,7 @@
             hid.append((Gather("y", lambda p, q, v=view: v(p, x, q)), [
                 Gather("x", lambda p, q, v=view, k=k: v(add(y, k), p, q)) for k in range(R)]))
     chunks = [Chunk(j) for j in range(len(CHUNKS))]
-    rowsum = take(4)
+    rowsum = take(7)
 
     loads[0].wait()
     go_gather.start()
@@ -285,45 +289,55 @@
         f.forward()
         f.near()
         s[1].start()
-        s[3].start()
     go_gather.forward()
     go_gather.finish()
     for c in loads[3:4] + loads[5:]:
         c.wait()
 
-    last = 8 + LAG * (len(CHUNKS) - 1)
-    for t in range(last + 1):
-        for j, chunk in enumerate(chunks):
-            if 0 <= t - LAG * j <= 8:
-                chunk.step(t - LAG * j)
-        if t == 0:
-            inp_gather.forward()
-        if t == 4:
-            inp_gather.finish()
-            inp_t[...] = inp_all[...].reshape(512, DS).T
+    def place(j, s):
+        return s + (LAG_SUM if s < 4 else LAG_GATHER) * j
+
+    def hid_near():
         for f, s in hid:
-            if t == last - FAR:
-                f.far()
-                s[2].start()
-            if t == last - 1:
-                for k in (0, 1, 3):
-                    s[k].forward()
-            if t == last:
-                s[2].forward()
-        for j, chunk in enumerate(chunks):
-            if t - LAG * j == 8:
-                chunk.step(9)
-                if t < last:
-                    chunk.weights()
-
-    rc(rowsum, acc.at[:, pl.ds(2 * (1 - core), 2)], sib, other).start()
+            s[3].start()
+
+    def hid_far():
+        for f, s in hid:
+            f.far()
+            s[2].start()
+
+    def hid_ahead():
+        for f, s in hid:
+            for k in (0, 1, 3):
+                s[k].forward()
+
+    def hid_last():
+        for f, s in hid:
+            s[2].forward()
+
+    def turn():
+        inp_gather.finish()
+        inp_t[...] = inp_all[...].reshape(512, DS).T
+
+    n = len(CHUNKS)
+    end = place(n - 1, 8)
+    plan = [(0.5, inp_gather.forward), (3.5, turn), (NEAR, hid_near)]
+    plan += [(end - AHEAD + 0.1, hid_ahead), (end - AHEAD - FAR, hid_far), (end + 0.1, hid_last), (end + 0.2, lambda: chunks[-1].step(9))]
+    for j, chunk in enumerate(chunks):
+        plan += [(place(j, s), lambda c=chunk, s=s: c.step(s)) for s in range(9)]
+        if j < n - 1:
+            plan += [(place(j, 8) + 0.3, lambda c=chunk: c.step(9)), (place(j, 8) + 0.3, chunk.weights)]
+    for _, act in sorted(plan, key=lambda v: v[0]):
+        act()
+
+    zout[...] = acc[...].reshape(R, 2, RB, DS).astype(BF16)
+    for i in range(3):
+        for j in range(2):
+            rc(rowsum + 1 + 2 * i + j, zout.at[add(z, i + 1), lax.rem(core + j, 2)], zin.at[i, j], zfar[i][j]).start()
+    rc(rowsum, acc.at[z, pl.ds(2 * (1 - core), 2)], sib, other).start()
     chunks[-1].weights()
     got(rowsum, sib)
-    for i in range(3):
-        p = add(z, i + 1)
-        zout[i] = (acc[p, pl.ds(2 * core, 2)] + sib[p]).reshape(RB, DS).astype(BF16)
-        rc(rowsum + 1 + i, zout.at[i], zin.at[i], zdev[i]).start()
-    total = (acc[z, pl.ds(2 * core, 2)] + sib[z]).reshape(RB, DS)
+    total = (acc[z, pl.ds(2 * core, 2)] + sib[...]).reshape(RB, DS)
     for f, s in hid:
         for g in s:
             g.near()
@@ -342,12 +356,13 @@
     for chunk in chunks:
         chunk.drain()
     for i in range(3):
-        got(rowsum + 1 + i, zin.at[i])
-        total = total + zin[i].astype(F32)
+        for j in range(2):
+            got(rowsum + 1 + 2 * i + j, zin.at[i, j])
+            total = total + zin[i, j].astype(F32)
     gi[...] = total.astype(BF16)
     sent(rowsum, sib)
-    for i in range(3):
-        sent(rowsum + 1 + i, zout.at[i])
+    for i in range(6):
+        sent(rowsum + 1 + i, zin.at[0, 0])
 
 
 def store_kernel(dg, du, dd, gi, dg_ref, du_ref, dd_ref, gi_ref, sem):
@@ -363,7 +378,7 @@
     anywhere = pl.BlockSpec(memory_space=pl.ANY)
     vmem = pl.BlockSpec(memory_space=pltpu.VMEM)
     shapes = ((DS, FFS), (DS, FFS), (FFS, DS), (RB, DS))
-    nsem = 14 + 60 + 48 * len(CHUNKS) + 4
+    nsem = 14 + 60 + 48 * len(CHUNKS) + 7
     dg, du, dd, gi = pl.pallas_call(
         comm_kernel,
         out_shape=[pltpu.VMEM(v, BF16) for v in shapes],
@@ -389,9 +404,9 @@
             pltpu.VMEM((2, 6, QR, HALF), BF16),
             pltpu.VMEM((2, 2, QR, HALF), BF16),
             pltpu.VMEM((R, R, TB, DS), F32),
-            pltpu.VMEM((R, 2, TB, DS), F32),
-            pltpu.VMEM((3, RB, DS), BF16),
-            pltpu.VMEM((3, RB, DS), BF16),
+            pltpu.VMEM((2, TB, DS), F32),
+            pltpu.VMEM((R, 2, RB, DS), BF16),
+            pltpu.VMEM((3, 2, RB, DS), BF16),
             pltpu.SemaphoreType.DMA((7,)),
             pltpu.SemaphoreType.DMA((nsem,)),
             pltpu.SemaphoreType.DMA((nsem,)),

time: 102 us -> 101 us (level)
  no operation moved by 1% of the time
where the time goes in v5:
time: 101 us
  Pallas kernels  100 us (99%)
    pallas_call x1, Pallas kernels, on_device(): pl.pallas_call(comm_kernel, out_shape=[pltpu.VMEM(v, BF16) for v in shape...  95.8 us
    pallas_call x1, Pallas kernels, on_device(): pl.pallas_call(store_kernel, out_shape=[jax.ShapeDtypeStruct(v, BF16) for...  4.29 us

profile of v5, /device:TPU:1, one launch (start us, length us, event | category | flops | bytes accessed | tf_op | source)
XLA Modules:
  0.0 100.7 jit_solution(11993394505514483510)
XLA Ops:
  0.6 95.8 %shard_map.102 = (bf16[512,3584]{1,0:T(8,128)(2,1)S(1)}, bf16[512,3584]{1,0:T(8,128)(2,1)S(1)}, bf16[3584,512]{1,0:T(8,128)(2,1)S(1)}, bf16[64,512]{1,0:T(8,128)(2,1)S(1)}) custom-call(bf16[64,512]{1,0:T(8,128)(2,1)} %inp_ref.1, bf16[64,512]{1,0:T(8,128)(2,1)} %go_ref.1, bf16[32,3584]{1,0:T(8,128)(2,1)} %gp_ref.1, bf16[32,3584]{1,0:T(8,128)(2,1)} %up_ref.1, ...), custom_call_target="tpu_custom_call" | custom-call | tf_op jit(solution)/shard_map/pallas_call | solution.py:382
  96.4 4.3 %shard_map.103 = (bf16[512,3584]{1,0:T(8,128)(2,1)}, bf16[512,3584]{1,0:T(8,128)(2,1)}, bf16[3584,512]{1,0:T(8,128)(2,1)}, bf16[64,512]{1,0:T(8,128)(2,1)}) custom-call(bf16[512,3584]{1,0:T(8,128)(2,1)S(1)} %get-tuple-element.12.dg, bf16[512,3584]{1,0:T(8,128)(2,1)S(1)} %get-tuple-element.13.du, bf16[3584,512]{1,0:T(8,128)(2,1)S(1)} %get-tuple-element.14.dd, ...), custom_call_target="tpu_custom_call" | custom-call | tf_op jit(solution)/shard_map/pallas_call | solution.py:419

commit v6 on v5

--- a/solution.py
+++ b/solution.py
@@ -274,8 +274,6 @@
 
     loads[0].wait()
     go_gather.start()
-    loads[4].wait()
-    inp_gather.start()
 
     loads[1].wait()
     loads[2].wait()
@@ -290,9 +288,10 @@
         f.near()
         s[1].start()
     go_gather.forward()
+    loads[4].wait()
+    inp_gather.start()
     go_gather.finish()
-    for c in loads[3:4] + loads[5:]:
-        c.wait()
+    loads[3].wait()
 
     def place(j, s):
         return s + (LAG_SUM if s < 4 else LAG_GATHER) * j
@@ -316,12 +315,14 @@
             s[2].forward()
 
     def turn():
+        loads[5].wait()
+        loads[6].wait()
         inp_gather.finish()
         inp_t[...] = inp_all[...].reshape(512, DS).T
 
     n = len(CHUNKS)
     end = place(n - 1, 8)
-    plan = [(0.5, inp_gather.forward), (3.5, turn), (NEAR, hid_near)]
+    plan = [(1.5, inp_gather.forward), (3.5, turn), (NEAR, hid_near)]
     plan += [(end - AHEAD + 0.1, hid_ahead), (end - AHEAD - FAR, hid_far), (end + 0.1, hid_last), (end + 0.2, lambda: chunks[-1].step(9))]
     for j, chunk in enumerate(chunks):
         plan += [(place(j, s), lambda c=chunk, s=s: c.step(s)) for s in range(9)]

time: 101 us -> 100 us (0.990)
  no operation moved by 1% of the time
where the time goes in v6:
time: 100 us
  Pallas kernels  99.7 us (100%)
    pallas_call x1, Pallas kernels, on_device(): pl.pallas_call(comm_kernel, out_shape=[pltpu.VMEM(v, BF16) for v in shape...  95.4 us
    pallas_call x1, Pallas kernels, on_device(): pl.pallas_call(store_kernel, out_shape=[jax.ShapeDtypeStruct(v, BF16) for...  4.29 us

profile of v6, /device:TPU:1, one launch (start us, length us, event | category | flops | bytes accessed | tf_op | source)
XLA Modules:
  0.0 100.3 jit_solution(3290168461903924828)
XLA Ops:
  0.6 95.4 %shard_map.102 = (bf16[512,3584]{1,0:T(8,128)(2,1)S(1)}, bf16[512,3584]{1,0:T(8,128)(2,1)S(1)}, bf16[3584,512]{1,0:T(8,128)(2,1)S(1)}, bf16[64,512]{1,0:T(8,128)(2,1)S(1)}) custom-call(bf16[64,512]{1,0:T(8,128)(2,1)} %inp_ref.1, bf16[64,512]{1,0:T(8,128)(2,1)} %go_ref.1, bf16[32,3584]{1,0:T(8,128)(2,1)} %gp_ref.1, bf16[32,3584]{1,0:T(8,128)(2,1)} %up_ref.1, ...), custom_call_target="tpu_custom_call" | custom-call | tf_op jit(solution)/shard_map/pallas_call | solution.py:383
  96.1 4.3 %shard_map.103 = (bf16[512,3584]{1,0:T(8,128)(2,1)}, bf16[512,3584]{1,0:T(8,128)(2,1)}, bf16[3584,512]{1,0:T(8,128)(2,1)}, bf16[64,512]{1,0:T(8,128)(2,1)}) custom-call(bf16[512,3584]{1,0:T(8,128)(2,1)S(1)} %get-tuple-element.12.dg, bf16[512,3584]{1,0:T(8,128)(2,1)S(1)} %get-tuple-element.13.du, bf16[3584,512]{1,0:T(8,128)(2,1)S(1)} %get-tuple-element.14.dd, ...), custom_call_target="tpu_custom_call" | custom-call | tf_op jit(solution)/shard_map/pallas_call | solution.py:420
